TPU v7x, 32 devices: a whole 2x2x4 slice. The times are simulated.
32 devices in a mesh: dp: 8 (over z, y), tp: 4 (over x, core).
Axes of the slice: x: 2, y: 2, z: 4, core: 2. Of those that a mesh axis runs over, the one named last changes fastest.
Arguments:
- tokens: bfloat16 [8, 2048, 768], P('dp', 'tp'), may hold values from -6 to 6
- cotangent: bfloat16 [8, 2048, 768], P('dp', 'tp'), may hold values from -6 to 6
- tags: int32 [8], P('dp'), may hold values from 0 to 7
- tag_weight: float32 [8], replicated, may hold values from 0.25 to 4
- query_weight: bfloat16 [768, 768], P(None, 'tp'), may hold values from -0.21875 to 0.21875
- key_value_weight: bfloat16 [768, 128], replicated, may hold values from -0.21875 to 0.21875
- output_weight: bfloat16 [768, 768], P('tp'), may hold values from -1.25 to 1.25
- up_weight: bfloat16 [768, 3072], P(None, 'tp'), may hold values from -0.21875 to 0.21875
- down_weight: bfloat16 [3072, 768], P('tp'), may hold values from -0.109375 to 0.109375
- norm_gain_one: float32 [768], replicated, may hold values from 0.25 to 1.75
- norm_bias_one: float32 [768], replicated, may hold values from -1.5 to 1.5
- norm_gain_two: float32 [768], replicated, may hold values from 0.25 to 1.75
- norm_bias_two: float32 [768], replicated, may hold values from -1.5 to 1.5
Outputs:
- block_out: bfloat16 [8, 2048, 768], P('dp', 'tp')
- grad_tokens: bfloat16 [8, 2048, 768], P('dp', 'tp')
- grad_query: float32 [768, 768], P(None, 'tp')
- grad_keyval: float32 [768, 128], replicated
- grad_output: float32 [768, 768], P('tp')
- grad_upward: float32 [768, 3072], P(None, 'tp')
- grad_downward: float32 [3072, 768], P('tp')
- grad_gain_one: float32 [768], replicated
- grad_bias_one: float32 [768], replicated
- grad_gain_two: float32 [768], replicated
- grad_bias_two: float32 [768], replicated
All inputs are finite; a program needn't handle non-finite values.
Results may differ from a plain program's by a relative error of at most 0.013.
Values may be sent and summed in bfloat16 or wider, within the bound.
A program may use at most 128 MiB of HBM per device.

v0:
```python
import jax
import jax.numpy as jnp
from jax import lax
from jax.sharding import PartitionSpec as P

HD = 64
ROT = 16


def layer_norm(values, gain_vec, shift_vec):
    row_mean = jnp.mean(values, axis=-1, keepdims=True)
    centred = values - row_mean
    variance = jnp.mean(centred * centred, axis=-1, keepdims=True)
    inverse = lax.rsqrt(variance + 1e-05)
    normal = centred * inverse
    return (normal * gain_vec + shift_vec, normal, inverse)


def norm_back(upstream, normal, inverse, gain_vec):
    scaled = upstream * gain_vec
    term_one = jnp.mean(scaled, axis=-1, keepdims=True)
    term_two = jnp.mean(scaled * normal, axis=-1, keepdims=True)
    return inverse * (scaled - term_one - normal * term_two)


def rot_angles(positions):
    frequencies = 10000.0 ** (-jnp.arange(0, ROT, 2, dtype=jnp.float32) / ROT)
    return positions.astype(jnp.float32)[:, None] * frequencies[None, :]


def rotate(values, angles, direction):
    half_rot = ROT // 2
    cosine = jnp.cos(angles)[:, None, :]
    sine_part = direction * jnp.sin(angles)[:, None, :]
    front_half = values[..., :half_rot]
    back_half = values[..., half_rot:ROT]
    return jnp.concatenate(
        [
            front_half * cosine - back_half * sine_part,
            back_half * cosine + front_half * sine_part,
            values[..., ROT:],
        ],
        axis=-1,
    )


def outer_sum(left, right):
    return lax.dot_general(
        left, right, (((0, 1), (0, 1)), ((), ())), preferred_element_type=jnp.float32
    )


def against(left, weight):
    return lax.dot_general(
        left, weight, (((2,), (1,)), ((), ())), preferred_element_type=jnp.float32
    )


def shards(
    tokens,
    cotangent,
    tags,
    tag_weight,
    query_weight,
    key_value_weight,
    output_weight,
    up_weight,
    down_weight,
    norm_gain_one,
    norm_bias_one,
    norm_gain_two,
    norm_bias_two,
):
    seq_dev, own_len, model_width = tokens.shape
    full_len = own_len * lax.axis_size("tp")
    heads_dev = query_weight.shape[1] // HD
    score_scale = HD ** (-0.5)
    block_rows = min(512, full_len)
    blocks = full_len // block_rows
    own_rows = tokens.astype(jnp.float32)
    full_angles = rot_angles(jnp.arange(full_len))
    first_normed, normal_one, inverse_one = layer_norm(own_rows, norm_gain_one, norm_bias_one)
    second_normed, normal_two, inverse_two = layer_norm(own_rows, norm_gain_two, norm_bias_two)
    low_one = first_normed.astype(jnp.bfloat16)
    low_two = second_normed.astype(jnp.bfloat16)
    rows_one, rows_two = (
        lax.all_gather(low_one, "tp", axis=1, tiled=True),
        lax.all_gather(low_two, "tp", axis=1, tiled=True),
    )
    key_value_rows = jnp.dot(rows_one, key_value_weight, preferred_element_type=jnp.float32)
    key_part = rotate(key_value_rows[:, :, None, :HD], full_angles, 1.0)[:, :, 0, :]
    key_value_rows = jnp.concatenate([key_part, key_value_rows[:, :, HD:]], axis=-1).astype(
        jnp.bfloat16
    )
    key_rows = key_value_rows[:, :, :HD]
    value_rows = key_value_rows[:, :, HD:]
    query_matrix = jnp.dot(rows_one, query_weight, preferred_element_type=jnp.float32).reshape(
        seq_dev, full_len, heads_dev, HD
    )
    query_matrix = rotate(query_matrix, full_angles, 1.0).astype(jnp.bfloat16)

    def block_scores(query_block, block_start):
        block_end = block_start + block_rows
        scores = (
            jnp.einsum(
                "sqhd,skd->sqhk",
                query_block,
                key_rows[:, :block_end],
                preferred_element_type=jnp.float32,
            )
            * score_scale
        )
        allowed = jnp.arange(block_end)[None, :] <= (block_start + jnp.arange(block_rows))[:, None]
        return jnp.where(allowed[None, :, None, :], scores, -1e30)

    context_list = []
    lse_list = []
    for block_index in range(blocks):
        block_start = block_index * block_rows
        block_end = block_start + block_rows
        scores = block_scores(query_matrix[:, block_start:block_end], block_start)
        row_top = jnp.max(scores, axis=-1, keepdims=True)
        weights = jnp.exp(scores - row_top)
        row_total = jnp.sum(weights, axis=-1, keepdims=True)
        weights_low = (weights / row_total).astype(jnp.bfloat16)
        context_list.append(
            jnp.einsum(
                "sqhk,skd->sqhd",
                weights_low,
                value_rows[:, :block_end],
                preferred_element_type=jnp.float32,
            )
        )
        lse_list.append(row_top + jnp.log(row_total))
    context_full = jnp.concatenate(context_list, axis=1)
    low_context = context_full.reshape(seq_dev, full_len, heads_dev * HD).astype(jnp.bfloat16)
    attention_branch = jnp.dot(low_context, output_weight, preferred_element_type=jnp.float32)
    hidden_rows = jnp.dot(rows_two, up_weight, preferred_element_type=jnp.float32)
    middle_rows = jax.nn.gelu(hidden_rows, approximate=False).astype(jnp.bfloat16)
    feedforward_branch = jnp.dot(middle_rows, down_weight, preferred_element_type=jnp.float32)
    branch = lax.psum_scatter(
        (attention_branch + feedforward_branch).astype(jnp.bfloat16),
        "tp",
        scatter_dimension=1,
        tiled=True,
    ).astype(jnp.float32)
    block_out = (own_rows + branch).astype(jnp.bfloat16)
    tag_ids = jnp.arange(tag_weight.shape[0], dtype=jnp.int32)
    row_weight = jnp.sum(
        jnp.where(tags[:, None] == tag_ids[None, :], tag_weight[None, :], 0.0), axis=1
    )
    upstream = cotangent.astype(jnp.float32) * row_weight[:, None, None]
    grad_rows = lax.all_gather(upstream.astype(jnp.bfloat16), "tp", axis=1, tiled=True)
    grad_output = outer_sum(low_context, grad_rows)
    grad_downward = outer_sum(middle_rows, grad_rows)
    grad_context = (
        against(grad_rows, output_weight)
        .astype(jnp.bfloat16)
        .reshape(seq_dev, full_len, heads_dev, HD)
    )
    grad_middle = against(grad_rows, down_weight)
    normal_cdf = 0.5 * (1.0 + lax.erf(hidden_rows * 0.7071067811865476))
    density = jnp.exp(-0.5 * hidden_rows * hidden_rows) * 0.3989422804014327
    grad_hidden = (grad_middle * (normal_cdf + hidden_rows * density)).astype(jnp.bfloat16)
    grad_upward = outer_sum(rows_two, grad_hidden)
    norm_part_two = against(grad_hidden, up_weight)
    grad_kv_full = jnp.zeros((seq_dev, full_len, 2 * HD), jnp.float32)
    query_grad_list = []
    for block_index in range(blocks):
        block_start = block_index * block_rows
        block_end = block_start + block_rows
        query_block = query_matrix[:, block_start:block_end]
        grad_block = grad_context[:, block_start:block_end]
        scores = block_scores(query_block, block_start)
        weights = jnp.exp(scores - lse_list[block_index])
        grad_weights = jnp.einsum(
            "sqhd,skd->sqhk",
            grad_block,
            value_rows[:, :block_end],
            preferred_element_type=jnp.float32,
        )
        row_delta = jnp.sum(
            grad_block.astype(jnp.float32) * context_list[block_index], axis=-1, keepdims=True
        )
        grad_scores = (weights * (grad_weights - row_delta)).astype(jnp.bfloat16)
        query_grad_list.append(
            jnp.einsum(
                "sqhk,skd->sqhd",
                grad_scores,
                key_rows[:, :block_end],
                preferred_element_type=jnp.float32,
            )
            * score_scale
        )
        grad_keys = (
            jnp.einsum(
                "sqhk,sqhd->skd", grad_scores, query_block, preferred_element_type=jnp.float32
            )
            * score_scale
        )
        grad_values = jnp.einsum(
            "sqhk,sqhd->skd",
            weights.astype(jnp.bfloat16),
            grad_block,
            preferred_element_type=jnp.float32,
        )
        grad_kv_full = grad_kv_full.at[:, :block_end].add(
            jnp.concatenate([grad_keys, grad_values], axis=-1)
        )
    grad_queries = jnp.concatenate(query_grad_list, axis=1)
    grad_queries = (
        rotate(grad_queries, full_angles, -1.0)
        .reshape(seq_dev, full_len, heads_dev * HD)
        .astype(jnp.bfloat16)
    )
    grad_query = outer_sum(rows_one, grad_queries)
    norm_part_one = against(grad_queries, query_weight)
    key_back = rotate(grad_kv_full[:, :, None, :HD], full_angles, -1.0)[:, :, 0, :]
    keyval_part = jnp.concatenate([key_back, grad_kv_full[:, :, HD:]], axis=-1)
    sum_one, sum_two, sum_keyval = (
        lax.psum_scatter(
            norm_part_one.astype(jnp.bfloat16), "tp", scatter_dimension=1, tiled=True
        ).astype(jnp.float32),
        lax.psum_scatter(
            norm_part_two.astype(jnp.bfloat16), "tp", scatter_dimension=1, tiled=True
        ).astype(jnp.float32),
        lax.psum_scatter(
            keyval_part.astype(jnp.bfloat16), "tp", scatter_dimension=1, tiled=True
        ).astype(jnp.float32),
    )
    low_keyval = sum_keyval.astype(jnp.bfloat16)
    grad_keyval = outer_sum(low_one, low_keyval)
    upstream_one = sum_one + against(low_keyval, key_value_weight)
    grad_gain_one = jnp.sum(upstream_one * normal_one, axis=(0, 1))
    grad_bias_one = jnp.sum(upstream_one, axis=(0, 1))
    grad_gain_two = jnp.sum(sum_two * normal_two, axis=(0, 1))
    grad_bias_two = jnp.sum(sum_two, axis=(0, 1))
    grad_tokens = (
        upstream
        + norm_back(upstream_one, normal_one, inverse_one, norm_gain_one)
        + norm_back(sum_two, normal_two, inverse_two, norm_gain_two)
    )
    grad_query, grad_output, grad_upward, grad_downward = lax.psum(
        (grad_query, grad_output, grad_upward, grad_downward), "dp"
    )
    grad_keyval, grad_gain_one, grad_bias_one, grad_gain_two, grad_bias_two = lax.psum(
        (grad_keyval, grad_gain_one, grad_bias_one, grad_gain_two, grad_bias_two), ("dp", "tp")
    )
    return (
        block_out,
        grad_tokens.astype(jnp.bfloat16),
        grad_query,
        grad_keyval,
        grad_output,
        grad_upward,
        grad_downward,
        grad_gain_one,
        grad_bias_one,
        grad_gain_two,
        grad_bias_two,
    )


def solution(mesh):
    in_specs = (
        P("dp", "tp", None),
        P("dp", "tp", None),
        P("dp"),
        P(),
        P(None, "tp"),
        P(),
        P("tp", None),
        P(None, "tp"),
        P("tp", None),
        P(),
        P(),
        P(),
        P(),
    )
    out_specs = (
        P("dp", "tp", None),
        P("dp", "tp", None),
        P(None, "tp"),
        P(),
        P("tp", None),
        P(None, "tp"),
        P("tp", None),
        P(),
        P(),
        P(),
        P(),
    )
    return jax.shard_map(shards, mesh=mesh, in_specs=in_specs, out_specs=out_specs, check_vma=False)
```

profile of v0, /device:TPU:0, one launch (start us, length us, event | category | flops | bytes accessed | tf_op | source)
XLA Modules:
  0.0 634.0 jit_solution(16872320583740692377)
XLA Ops:
  21.1 23.4 %all-gather.4.cloned.1.call-done = bf16[1,2048,768]{2,1,0:T(8,128)(2,1)} async-done(((bf16[1,512,768]{2,1,0:T(8,128)(2,1)}), bf16[1,2048,768]{2,1,0:T(8,128)(2,1)}) %all-gather.4.cloned.1.call-update) | async-done | bytes 3145744 | tf_op jit(solution)/shard_map/all_gather | solution.py:87
  44.5 3.2 fusion.186
  66.5 5.9 fusion.4
  72.3 6.7 %fusion = f32[512,3]{0,1:T(4,128)S(1)} fusion(f32[512,3,2048]{2,0,1:T(8,128)} %get-tuple-element.114, f32[512,3]{0,1:T(4,128)S(1)} %get-tuple-element.113, pred[512,2048]{1,0:T(8,128)(4,1)S(1)} %iota_compare_fusion), kind=kLoop, calls=%fused_computation.5 | loop fusion | flops 12581376 | bytes 13643776 | tf_op jit(solution)/shard_map/reduce_sum | solution.py:124
  79.1 7.8 %fusion.188 = (bf16[512,3,64]{0,2,1:T(8,128)(2,1)}, f32[512,3,64]{0,2,1:T(8,128)}) fusion(bf16[1,2048,128]{1,2,0:T(8,128)(2,1)S(1)} %get-tuple-element.107, f32[512,3,2048]{2,0,1:T(8,128)} %get-tuple-element.114, f32[512,3]{0,1:T(4,128)S(1)} %fusion, f32[512,3]{0,1:T(4,128)S(1)} %get-tuple-element.113, pred[512,2048]{1,0:T(8,128)(4,1)S(1)} %iota_compare_fusion), kind=kOutput, calls=%fused_computation.286 | convolution fusion | flops 418480128 | bytes 14499840 | tf_op jit(solution)/shard_map/sqhk,skd->sqhd/dot_general | solution.py:127
  91.0 3.2 fusion.61
  107.0 8.8 %multiply_convert_fusion = bf16[512,3,2048]{2,0,1:T(8,128)(2,1)S(1)} fusion(f32[512,3,2048]{2,0,1:T(8,128)} %get-tuple-element.114, f32[512,3]{0,1:T(4,128)S(1)} %get-tuple-element.80, f32[512,3]{0,1:T(4,128)S(1)} %copy-done.48, pred[512,2048]{1,0:T(8,128)(4,1)S(1)} %iota_compare_fusion, bf16[1,2048,128]{1,2,0:T(8,128)(2,1)S(1)} %copy-done.20, ...), kind=kOutput, calls=%fused_computation | convolution fusion | flops 421527552 | bytes 20398080 | tf_op jit(solution)/shard_map/sqhd,skd->sqhk/dot_general | solution.py:176
  120.3 6.4 %fusion.70 = f32[1,2048,64]{1,2,0:T(8,128)S(1)} fusion(f32[512,3,2048]{2,0,1:T(8,128)} %get-tuple-element.114, f32[512,3]{0,1:T(4,128)S(1)} %copy-done.48, pred[512,2048]{1,0:T(8,128)(4,1)S(1)} %iota_compare_fusion, bf16[1,2048,3,64]{1,3,2,0:T(8,128)(2,1)S(1)} %bitcast.283), kind=kOutput, calls=%fused_computation.100 | convolution fusion | flops 415236096 | bytes 14360576 | tf_op jit(solution)/shard_map/sqhk,sqhd->skd/dot_general | solution.py:201
  128.7 17.5 %fusion.7 = (bf16[2048,768]{1,0:T(8,128)(2,1)}, f32[2048,768]{1,0:T(8,128)S(1)}) fusion(bf16[768,768]{1,0:T(8,128)(2,1)S(1)} %copy-done, bf16[1,2048,768]{2,1,0:T(8,128)(2,1)} %all-gather.6.cloned.1.call-done), kind=kOutput, calls=%fused_computation.19 | convolution fusion | flops 2518155264 | bytes 13762560 | tf_op jit(solution)/shard_map/dot_general | solution.py:138
  146.3 5.2 fusion.13
  153.2 4.0 fusion.54
  162.7 4.0 fusion.115
  171.8 4.9 fusion.191
  179.8 3.6 fusion.34
  183.6 4.2 fusion.39
  187.8 4.2 fusion.32
  194.2 3.6 fusion.47
  197.9 37.9 %reduce-scatter.7.cloned.1.call-done = bf16[1,512,768]{2,1,0:T(8,128)(2,1)} async-done(((bf16[1,2048,768]{2,1,0:T(8,128)(2,1)}), bf16[1,512,768]{2,1,0:T(8,128)(2,1)}) %reduce-scatter.7.cloned.1.call-update) | async-done | bytes 786448 | tf_op jit(solution)/shard_map/reduce_scatter | solution.py:221
  235.8 4.6 fusion.100
  240.4 40.1 %all-reduce.1 = (f32[768]{0:T(1024)}, f32[768]{0:T(1024)}, f32[768]{0:T(1024)}, f32[768]{0:T(1024)}) all-reduce(f32[768]{0:T(1024)} %get-tuple-element.67, f32[768]{0:T(1024)} %get-tuple-element.72, f32[768]{0:T(1024)} %get-tuple-element.74, f32[768]{0:T(1024)} %get-tuple-element.76), channel_id=1, replica_groups=mesh['dp'=8,'tp'=4] {'dp','tp'}, use_global_device_ids=true, to_apply=%region_29.30 | all-reduce | flops 3072 | bytes 24576 | tf_op jit(solution)/shard_map/psum | solution.py:246
  283.0 4.0 fusion.97
  287.0 122.9 %all-reduce.6.cloned.1.call-done = f32[768,128]{1,0:T(8,128)} async-done(((f32[768,128]{1,0:T(8,128)}), f32[768,128]{1,0:T(8,128)}) %all-reduce.6.cloned.1.call-update) | async-done | bytes 393232 | tf_op jit(solution)/shard_map/psum | solution.py:246
  410.0 206.7 %all-reduce.8.cloned.1.call-done = (f32[768,192]{0,1:T(8,128)}, f32[192,768]{1,0:T(8,128)}, f32[768,768]{1,0:T(8,128)}, f32[768,768]{1,0:T(8,128)}) async-done(((f32[768,192]{0,1:T(8,128)}, f32[192,768]{1,0:T(8,128)}, f32[768,768]{1,0:T(8,128)}, f32[768,768]{1,0:T(8,128)}), (f32[768,192]{0,1:T(8,128)}, f32[192,768]{1,0:T(8,128)}, f32[768,768]{1,0:T(8,128)}, ...) | async-done | bytes 5898256 | tf_op jit(solution)/shard_map/psum | solution.py:243
  622.4 3.2 copy.45
  (241 shorter events, 81.7 us)
Async XLA Ops:
  7.2 121.6 %copy-start = (bf16[768,768]{1,0:T(8,128)(2,1)S(1)}, bf16[768,768]{1,0:T(8,128)(2,1)}, u32[]{:S(2)}) copy-start(bf16[768,768]{1,0:T(8,128)(2,1)} %param.30) | copy-start | bytes 3538948
  7.2 37.3 %all-gather.4.cloned.1.call-start = ((), (), s32[]{:S(2)}) async-start(), calls=%async_computation.4 | async-start | bytes 3932160 | tf_op jit(solution)/shard_map/all_gather | solution.py:87
  10.2 34.3 %copy-start.32 = (bf16[768,128]{1,0:T(8,128)(2,1)S(1)}, bf16[768,128]{1,0:T(8,128)(2,1)}, u32[]{:S(2)}) copy-start(bf16[768,128]{1,0:T(8,128)(2,1)} %param.28) | copy-start | bytes 589828
  13.1 77.8 %all-gather.8.cloned.1.call-start = ((), (), s32[]{:S(2)}) async-start(), calls=%async_computation.7 | async-start | bytes 3932160 | tf_op jit(solution)/shard_map/all_gather | solution.py:153
  16.1 112.6 %all-gather.6.cloned.1.call-start = ((), (), s32[]{:S(2)}) async-start(), calls=%async_computation.5 | async-start | bytes 3932160 | tf_op jit(solution)/shard_map/all_gather | solution.py:88
  16.8 175.2 %reduce-scatter.9.cloned.1.call-start = ((), (), s32[]{:S(2)}) async-start(), calls=%async_computation.9 | async-start | bytes 655360 | tf_op jit(solution)/shard_map/reduce_scatter | solution.py:227
  16.9 33.4 %copy-start.50 = (f32[8]{0:T(128)}, f32[8]{0:T(128)S(1)}, u32[]{:S(2)}) copy-start(f32[8]{0:T(128)S(1)} %multiply_power_fusion) | copy-start | bytes 100
  21.1 29.3 %copy-start.21 = (f32[2048,8]{0,1:T(8,128)}, f32[2048,8]{0,1:T(8,128)S(1)}, u32[]{:S(2)}) copy-start(f32[2048,8]{0,1:T(8,128)S(1)} %get-tuple-element.104) | copy-start | bytes 196612
  47.7 31.4 %copy-start.19 = (bf16[1,2048,128]{1,2,0:T(8,128)(2,1)}, bf16[1,2048,128]{1,2,0:T(8,128)(2,1)S(1)}, u32[]{:S(2)}) copy-start(bf16[1,2048,128]{1,2,0:T(8,128)(2,1)S(1)} %get-tuple-element.107) | copy-start | bytes 1572868
  47.8 18.7 %copy-start.15 = (bf16[1,2048,1,48]{1,3,2,0:T(8,128)(2,1)}, bf16[1,2048,1,48]{1,3,2,0:T(8,128)(2,1)S(1)}, u32[]{:S(2)}) copy-start(bf16[1,2048,1,48]{1,3,2,0:T(8,128)(2,1)S(1)} %slice.370) | copy-start | bytes 589828
  48.1 18.3 %copy-start.26 = (bf16[1,2048,1,8]{1,3,2,0:T(8,128)(2,1)}, bf16[1,2048,1,8]{1,3,2,0:T(8,128)(2,1)S(1)}, u32[]{:S(2)}) copy-start(bf16[1,2048,1,8]{1,3,2,0:T(8,128)(2,1)S(1)} %get-tuple-element.100) | copy-start | bytes 98308
  50.5 37.0 %copy-start.17 = (bf16[1,2048,64]{1,2,0:T(8,128)(2,1)}, bf16[1,2048,64]{1,2,0:T(8,128)(2,1)S(1)}, u32[]{:S(2)}) copy-start(bf16[1,2048,64]{1,2,0:T(8,128)(2,1)S(1)} %fusion.184) | copy-start | bytes 786436
  128.7 69.2 %reduce-scatter.11.cloned.1.call-start = ((), (), s32[]{:S(2)}) async-start(), calls=%async_computation.10 | async-start | bytes 3932160 | tf_op jit(solution)/shard_map/reduce_scatter | solution.py:224
  157.3 78.5 %reduce-scatter.7.cloned.1.call-start = ((), (), s32[]{:S(2)}) async-start(), calls=%async_computation.8 | async-start | bytes 3932160 | tf_op jit(solution)/shard_map/reduce_scatter | solution.py:221
  171.7 111.3 %reduce-scatter.5.cloned.1.call-start = ((), (), s32[]{:S(2)}) async-start(), calls=%async_computation.6 | async-start | bytes 3932160 | tf_op jit(solution)/shard_map/reduce_scatter | solution.py:141
  179.5 230.5 %all-reduce.6.cloned.1.call-start = ((), (), s32[]{:S(2)}) async-start(), calls=%async_computation.11 | async-start | bytes 786432 | tf_op jit(solution)/shard_map/psum | solution.py:246
  194.1 41.7 %copy-start.9 = (bf16[1,512,768]{2,1,0:T(8,128)(2,1)S(1)}, bf16[1,512,768]{2,1,0:T(8,128)(2,1)}, u32[]{:S(2)}) copy-start(bf16[1,512,768]{2,1,0:T(8,128)(2,1)} %param.23) | copy-start | bytes 2359300
  194.1 41.7 %copy-start.39 = (f32[512]{0:T(512)S(1)}, f32[512]{0:T(512)}, u32[]{:S(2)}) copy-start(f32[512]{0:T(512)} %copy-done.38) | copy-start | bytes 6148
  194.1 41.7 %copy-start.45 = (f32[512]{0:T(512)S(1)}, f32[512]{0:T(512)}, u32[]{:S(2)}) copy-start(f32[512]{0:T(512)} %copy-done.44) | copy-start | bytes 6148
  194.1 41.7 %copy-start.46 = (f32[768]{0:T(1024)S(1)}, f32[768]{0:T(1024)}, u32[]{:S(2)}) copy-start(f32[768]{0:T(1024)} %param.32) | copy-start | bytes 9220
  194.1 41.7 %copy-start.47 = (f32[768]{0:T(1024)S(1)}, f32[768]{0:T(1024)}, u32[]{:S(2)}) copy-start(f32[768]{0:T(1024)} %param.34) | copy-start | bytes 9220
  194.1 422.5 %all-reduce.8.cloned.1.call-start = ((), (), s32[]{:S(2)}) async-start(), calls=%async_computation.12 | async-start | bytes 11796480 | tf_op jit(solution)/shard_map/psum | solution.py:243
  197.8 85.2 %copy-start.13 = (bf16[1,512,768]{2,1,0:T(8,128)(2,1)S(1)}, bf16[1,512,768]{2,1,0:T(8,128)(2,1)}, u32[]{:S(2)}) copy-start(bf16[1,512,768]{2,1,0:T(8,128)(2,1)} %param.24) | copy-start | bytes 2359300
  197.9 85.2 %copy-start.24 = (bf16[1,512,768]{2,1,0:T(8,128)(2,1)S(1)}, bf16[1,512,768]{2,1,0:T(8,128)(2,1)}, u32[]{:S(2)}) copy-start(bf16[1,512,768]{2,1,0:T(8,128)(2,1)} %reduce-scatter.11.cloned.1.call-done) | copy-start | bytes 2359300
  (56 other events, 288.4 us)
Sparse Core Ops, SparseCore 0:
  13.2 31.2 all-gather.3
  46.6 28.5 all-gather.7
  77.4 28.5 all-gather.5
  128.8 21.6 reduce-scatter.8
  157.4 37.9 reduce-scatter.10
  197.8 37.9 reduce-scatter.6
  238.5 38.1 reduce-scatter.4
  282.6 127.3 all-reduce.5
  415.1 201.4 all-reduce.7
where the time goes:
time: 640 us; the launch traced here: 634 us
  waiting for transfers between devices  392 us (61%)
  matrix products  132 us (21%)
  blocking collectives  40.1 us (6%)
  other arithmetic  33.5 us (5%)
  local copies, waits for them, and re-layouts  19.8 us (3%)
  between operations  16.1 us (3%)
    psum x1, waiting for transfers between devices, shards(): lax.psum((grad_query, grad_output, grad_upward, grad_downward), 'dp')  207 us
    psum x1, waiting for transfers between devices, shards(): lax.psum((grad_keyval, grad_gain_one, grad_bias_one, grad_gain_two, grad_...  123 us
    psum x1, blocking collectives, shards(): lax.psum((grad_keyval, grad_gain_one, grad_bias_one, grad_gain_two, grad_...  40.1 us
    reduce_scatter x1, waiting for transfers between devices, shards(): lax.psum_scatter(norm_part_one.astype(jnp.bfloat16), 'tp', scatter_dimens...  37.9 us
    all_gather x1, waiting for transfers between devices, shards(): lax.all_gather(low_one, 'tp', axis=1, tiled=True)  23.4 us
    dot_general x5, matrix products, against(): lax.dot_general(left, weight, (((2,), (1,)), ((), ())), preferred_element...  19.8 us
    unnamed x147, local copies, waits for them, and re-layouts  19.6 us
    dot_general x5, matrix products, outer_sum(): lax.dot_general(left, right, (((0, 1), (0, 1)), ((), ())), preferred_elem...  17.6 us
  transfers between devices with their start and end apart: 9, of which 4 were waited for; matrix products, arithmetic and copies ran while one was open for 25% of the time, Pallas kernels for 0%

commit v1 on v0

--- a/solution.py
+++ b/solution.py
@@ -16,8 +16,7 @@
     return (normal * gain_vec + shift_vec, normal, inverse)
 
 
-def norm_back(upstream, normal, inverse, gain_vec):
-    scaled = upstream * gain_vec
+def norm_back(scaled, normal, inverse):
     term_one = jnp.mean(scaled, axis=-1, keepdims=True)
     term_two = jnp.mean(scaled * normal, axis=-1, keepdims=True)
     return inverse * (scaled - term_one - normal * term_two)
@@ -79,14 +78,16 @@
     blocks = full_len // block_rows
     own_rows = tokens.astype(jnp.float32)
     full_angles = rot_angles(jnp.arange(full_len))
-    first_normed, normal_one, inverse_one = layer_norm(own_rows, norm_gain_one, norm_bias_one)
-    second_normed, normal_two, inverse_two = layer_norm(own_rows, norm_gain_two, norm_bias_two)
-    low_one = first_normed.astype(jnp.bfloat16)
-    low_two = second_normed.astype(jnp.bfloat16)
-    rows_one, rows_two = (
-        lax.all_gather(low_one, "tp", axis=1, tiled=True),
-        lax.all_gather(low_two, "tp", axis=1, tiled=True),
-    )
+    tag_ids = jnp.arange(tag_weight.shape[0], dtype=jnp.int32)
+    row_weight = jnp.sum(
+        jnp.where(tags[:, None] == tag_ids[None, :], tag_weight[None, :], 0.0), axis=1
+    )
+    upstream = cotangent.astype(jnp.float32) * row_weight[:, None, None]
+    all_rows = lax.all_gather(tokens, "tp", axis=1, tiled=True).astype(jnp.float32)
+    grad_rows = lax.all_gather(upstream.astype(jnp.bfloat16), "tp", axis=1, tiled=True)
+    normed_one, normal_all, _ = layer_norm(all_rows, norm_gain_one, norm_bias_one)
+    rows_one = normed_one.astype(jnp.bfloat16)
+    rows_two = (normal_all * norm_gain_two + norm_bias_two).astype(jnp.bfloat16)
     key_value_rows = jnp.dot(rows_one, key_value_weight, preferred_element_type=jnp.float32)
     key_part = rotate(key_value_rows[:, :, None, :HD], full_angles, 1.0)[:, :, 0, :]
     key_value_rows = jnp.concatenate([key_part, key_value_rows[:, :, HD:]], axis=-1).astype(
@@ -145,12 +146,6 @@
         tiled=True,
     ).astype(jnp.float32)
     block_out = (own_rows + branch).astype(jnp.bfloat16)
-    tag_ids = jnp.arange(tag_weight.shape[0], dtype=jnp.int32)
-    row_weight = jnp.sum(
-        jnp.where(tags[:, None] == tag_ids[None, :], tag_weight[None, :], 0.0), axis=1
-    )
-    upstream = cotangent.astype(jnp.float32) * row_weight[:, None, None]
-    grad_rows = lax.all_gather(upstream.astype(jnp.bfloat16), "tp", axis=1, tiled=True)
     grad_output = outer_sum(low_context, grad_rows)
     grad_downward = outer_sum(middle_rows, grad_rows)
     grad_context = (
@@ -217,35 +212,43 @@
     norm_part_one = against(grad_queries, query_weight)
     key_back = rotate(grad_kv_full[:, :, None, :HD], full_angles, -1.0)[:, :, 0, :]
     keyval_part = jnp.concatenate([key_back, grad_kv_full[:, :, HD:]], axis=-1)
-    sum_one, sum_two, sum_keyval = (
-        lax.psum_scatter(
-            norm_part_one.astype(jnp.bfloat16), "tp", scatter_dimension=1, tiled=True
-        ).astype(jnp.float32),
-        lax.psum_scatter(
-            norm_part_two.astype(jnp.bfloat16), "tp", scatter_dimension=1, tiled=True
-        ).astype(jnp.float32),
-        lax.psum_scatter(
-            keyval_part.astype(jnp.bfloat16), "tp", scatter_dimension=1, tiled=True
-        ).astype(jnp.float32),
-    )
-    low_keyval = sum_keyval.astype(jnp.bfloat16)
-    grad_keyval = outer_sum(low_one, low_keyval)
-    upstream_one = sum_one + against(low_keyval, key_value_weight)
-    grad_gain_one = jnp.sum(upstream_one * normal_one, axis=(0, 1))
-    grad_bias_one = jnp.sum(upstream_one, axis=(0, 1))
-    grad_gain_two = jnp.sum(sum_two * normal_two, axis=(0, 1))
-    grad_bias_two = jnp.sum(sum_two, axis=(0, 1))
-    grad_tokens = (
-        upstream
-        + norm_back(upstream_one, normal_one, inverse_one, norm_gain_one)
-        + norm_back(sum_two, normal_two, inverse_two, norm_gain_two)
-    )
-    grad_query, grad_output, grad_upward, grad_downward = lax.psum(
-        (grad_query, grad_output, grad_upward, grad_downward), "dp"
-    )
-    grad_keyval, grad_gain_one, grad_bias_one, grad_gain_two, grad_bias_two = lax.psum(
-        (grad_keyval, grad_gain_one, grad_bias_one, grad_gain_two, grad_bias_two), ("dp", "tp")
-    )
+    low_keyval = keyval_part.astype(jnp.bfloat16)
+    grad_keyval = outer_sum(rows_one, low_keyval)
+    part_one = norm_part_one + against(low_keyval, key_value_weight)
+    small = jnp.stack(
+        [
+            jnp.sum(part_one * normal_all, axis=(0, 1)),
+            jnp.sum(part_one, axis=(0, 1)),
+            jnp.sum(norm_part_two * normal_all, axis=(0, 1)),
+            jnp.sum(norm_part_two, axis=(0, 1)),
+        ]
+    )
+    scaled = lax.psum_scatter(
+        (part_one * norm_gain_one + norm_part_two * norm_gain_two).astype(jnp.bfloat16),
+        "tp",
+        scatter_dimension=1,
+        tiled=True,
+    ).astype(jnp.float32)
+    _, normal_own, inverse_own = layer_norm(own_rows, norm_gain_one, norm_bias_one)
+    grad_tokens = upstream + norm_back(scaled, normal_own, inverse_own)
+    grad_query, grad_output, grad_upward, grad_downward = [
+        v.astype(jnp.float32)
+        for v in lax.psum(
+            tuple(
+                v.astype(jnp.bfloat16)
+                for v in (grad_query, grad_output, grad_upward, grad_downward)
+            ),
+            "dp",
+        )
+    ]
+    tail = lax.psum(
+        jnp.concatenate([grad_keyval.reshape(-1), small.reshape(-1)]).reshape(-1, 128), ("dp", "tp")
+    ).reshape(-1)
+    grad_keyval, small = (
+        tail[: grad_keyval.size].reshape(grad_keyval.shape),
+        tail[grad_keyval.size :].reshape(small.shape),
+    )
+    grad_gain_one, grad_bias_one, grad_gain_two, grad_bias_two = small
     return (
         block_out,
         grad_tokens.astype(jnp.bfloat16),

time: 640 us -> 517 us (0.81)
  waiting for transfers between devices: 392 us -> 324 us
  blocking collectives: 40.1 us -> 0 us
  matrix products: 132 us -> 111 us
  other arithmetic: 33.5 us -> 49.1 us
  local copies, waits for them, and re-layouts: 19.8 us -> 11.6 us
    psum x2, waiting for transfers between devices: 330 us -> 230 us  [the longest x1 128 us: shards(): lax.psum(tuple((v.astype(jnp.bfloat16) for v in (grad_query, grad_output,...]
    psum x1 -> x0, blocking collectives: 40.1 us -> none  [shards(): lax.psum((grad_keyval, grad_gain_one, grad_bias_one, grad_gain_two, grad_...]
    reduce_scatter x1, waiting for transfers between devices: 0.01 us -> 38.7 us  [shards(): lax.psum_scatter((attention_branch + feedforward_branch).astype(jnp.bfloa...]
    unnamed x147 -> x158, local copies, waits for them, and re-layouts: 19.6 us -> 8.26 us
    reduce_scatter x3 -> x1, waiting for transfers between devices: 37.9 us -> 29.9 us  [shards(): lax.psum_scatter((part_one * norm_gain_one + norm_part_two * norm_gain_tw...]
    convert_element_type x1 -> x5, other arithmetic: 2.85 us -> 10.8 us  [the longest x4 9.36 us: shards(): v.astype(jnp.float32)]
    all_gather x2 -> x1, waiting for transfers between devices: 23.4 us -> 23.9 us  [shards(): lax.all_gather(tokens, 'tp', axis=1, tiled=True).astype(jnp.float32)]
  transfers between devices with their start and end apart: 9 -> 6, of which waited for: 4 -> 5; matrix products, arithmetic and copies ran while one was open for 25% -> 17% of each run, Pallas kernels for 0% -> 0%
where the time goes in v1:
time: 517 us; the launch traced here: 513 us
  waiting for transfers between devices  324 us (63%)
  matrix products  111 us (21%)
  other arithmetic  49.1 us (9%)
  between operations  16.2 us (3%)
  local copies, waits for them, and re-layouts  11.6 us (2%)
    psum x1, waiting for transfers between devices, shards(): lax.psum(tuple((v.astype(jnp.bfloat16) for v in (grad_query, grad_output,...  128 us
    psum x1, waiting for transfers between devices, shards(): lax.psum(jnp.concatenate([grad_keyval.reshape(-1), small.reshape(-1)]).re...  103 us
    reduce_scatter x1, waiting for transfers between devices, shards(): lax.psum_scatter((attention_branch + feedforward_branch).astype(jnp.bfloa...  38.7 us
    reduce_scatter x1, waiting for transfers between devices, shards(): lax.psum_scatter((part_one * norm_gain_one + norm_part_two * norm_gain_tw...  29.9 us
    all_gather x1, waiting for transfers between devices, shards(): lax.all_gather(tokens, 'tp', axis=1, tiled=True).astype(jnp.float32)  23.9 us
    dot_general x1, matrix products, shards(): jnp.dot(rows_two, up_weight, preferred_element_type=jnp.float32)  17.6 us
    dot_general x5, matrix products, against(): lax.dot_general(left, weight, (((2,), (1,)), ((), ())), preferred_element...  15 us
    dot_general x5, matrix products, outer_sum(): lax.dot_general(left, right, (((0, 1), (0, 1)), ((), ())), preferred_elem...  14.9 us
  transfers between devices with their start and end apart: 6, of which 5 were waited for; matrix products, arithmetic and copies ran while one was open for 17% of the time, Pallas kernels for 0%

profile of v1, /device:TPU:0, one launch (start us, length us, event | category | flops | bytes accessed | tf_op | source)
XLA Modules:
  0.0 513.2 jit_solution(20159249226310110)
XLA Ops:
  17.0 23.9 %all-gather.3.cloned.1.call-done = bf16[1,2048,768]{2,1,0:T(8,128)(2,1)} async-done(((bf16[1,512,768]{2,1,0:T(8,128)(2,1)}), bf16[1,2048,768]{2,1,0:T(8,128)(2,1)}) %all-gather.3.cloned.1.call-update) | async-done | bytes 3145744 | tf_op jit(solution)/shard_map/all_gather | solution.py:86
  43.4 2.9 fusion.17
  61.7 6.2 %fusion.10 = (f32[512,3]{0,1:T(4,128)S(1)}, f32[512,3,2048]{2,0,1:T(8,128)}) fusion(pred[512,2048]{1,0:T(8,128)(4,1)S(1)} %iota_compare_fusion, bf16[1,2048,1,48]{1,3,2,0:T(8,128)(2,1)S(1)} %slice.387, bf16[1,2048,1,8]{1,3,2,0:T(8,128)(2,1)S(1)} %get-tuple-element.92, bf16[1,2048,1,8]{1,3,2,0:T(8,128)(2,1)S(1)} %get-tuple-element.91, ...), kind=kOutput, calls=%fused_computation.25 | convolution fusion | flops 412875264 | bytes 14096384 | tf_op jit(solution)/shard_map/sqhd,skd->sqhk/dot_general | solution.py:106
  70.5 6.9 %fusion = f32[512,3]{0,1:T(4,128)S(1)} fusion(f32[512,3,2048]{2,0,1:T(8,128)} %get-tuple-element.109, f32[512,3]{0,1:T(4,128)S(1)} %get-tuple-element.108, pred[512,2048]{1,0:T(8,128)(4,1)S(1)} %iota_compare_fusion), kind=kLoop, calls=%fused_computation.6 | loop fusion | flops 12581376 | bytes 13643776 | tf_op jit(solution)/shard_map/reduce_sum | solution.py:125
  78.6 3.1 fusion.194
  82.2 2.9 fusion.193
  86.2 4.8 fusion.192
  91.0 3.1 fusion.71
  94.2 7.3 %fusion.80 = f32[1,2048,64]{1,2,0:T(8,128)} fusion(f32[512,3,2048]{2,0,1:T(8,128)} %get-tuple-element.109, f32[512,3]{0,1:T(4,128)S(1)} %copy-done.50, pred[512,2048]{1,0:T(8,128)(4,1)S(1)} %iota_compare_fusion, bf16[1,2048,3,64]{1,3,2,0:T(8,128)(2,1)S(1)} %bitcast.290), kind=kOutput, calls=%fused_computation.113 | convolution fusion | flops 415236096 | bytes 14360576 | tf_op jit(solution)/shard_map/sqhk,sqhd->skd/dot_general | solution.py:196
  104.4 4.6 multiply_convert_fusion
  130.1 17.6 %fusion.20 = (bf16[2048,768]{1,0:T(8,128)(2,1)}, f32[2048,768]{1,0:T(8,128)S(1)}) fusion(bf16[768,768]{1,0:T(8,128)(2,1)S(1)} %copy-done, bf16[1,2048,768]{2,1,0:T(8,128)(2,1)S(1)} %copy-done.3, f32[768]{0:T(1024)S(1)} %copy-done.59, f32[768]{0:T(1024)S(1)} %copy-done.55, f32[2048]{0:T(1024)S(1)} %copy-done.40, f32[2048]{0:T(1024)S(1)} %broadcast_multiply_fusion.1), kind=kOutput, calls=%fused_computation.35 | convolution fusion | flops 2527592448 | bytes 13785088 | tf_op jit(solution)/shard_map/dot_general | solution.py:139
  147.7 5.2 %fusion.26 = bf16[2048,768]{1,0:T(8,128)(2,1)S(1)} fusion(f32[2048,768]{1,0:T(8,128)S(1)} %get-tuple-element.112, bf16[768,768]{1,0:T(8,128)(2,1)S(1)} %copy-done.58, bf16[1,2048,768]{2,1,0:T(8,128)(2,1)S(1)} %copy-done.56), kind=kOutput, calls=%fused_computation.41 | convolution fusion | flops 2431647744 | bytes 13762560 | tf_op jit(solution)/shard_map/dot_general | solution.py:53
  158.8 3.0 fusion.15
  161.8 2.9 fusion.188
  165.8 7.1 %convolution_convert_fusion = bf16[768,768]{1,0:T(8,128)(2,1)} fusion(bf16[2048,768]{1,0:T(8,128)(2,1)} %copy-done.61, bf16[1,2048,768]{2,1,0:T(8,128)(2,1)} %all-gather.3.cloned.1.call-done, f32[768]{0:T(1024)S(1)} %copy-done.59, f32[768]{0:T(1024)S(1)} %copy-done.55, f32[2048]{0:T(1024)S(1)} %copy-done.40, f32[2048]{0:T(1024)S(1)} %broadcast_multiply_fusion.1), kind=kOutput, calls=%fused_computation.143 | convolution fusion | flops 2425946112 | bytes 7493632 | tf_op jit(solution)/shard_map/dot_general | solution.py:47
  173.0 3.7 fusion.104
  180.6 4.9 fusion.195
  188.8 102.7 %all-reduce.5.cloned.1.call-done = f32[792,128]{1,0:T(8,128)} async-done(((f32[792,128]{1,0:T(8,128)}), f32[792,128]{1,0:T(8,128)}) %all-reduce.5.cloned.1.call-update) | async-done | bytes 405520 | tf_op jit(solution)/shard_map/psum | solution.py:244
  294.7 127.7 %all-reduce.7.cloned.1.call-done = (bf16[768,192]{0,1:T(8,128)(2,1)}, bf16[192,768]{1,0:T(8,128)(2,1)}, bf16[768,768]{1,0:T(8,128)(2,1)}, bf16[768,768]{1,0:T(8,128)(2,1)}) async-done(((bf16[768,192]{0,1:T(8,128)(2,1)}, bf16[192,768]{1,0:T(8,128)(2,1)}, bf16[768,768]{1,0:T(8,128)(2,1)}, bf16[768,768]{1,0:T(8,128)(2,1)}), (bf16[768,192]{0,1:T(8,128)(2,1)}, bf16[192,768]{1,0:T(8,128)(2,1)}, ...) | async-done | bytes 2949136 | tf_op jit(solution)/shard_map/psum | solution.py:236
  426.1 2.8 convert_element_type.267
  428.9 2.9 convert_element_type.269
  431.8 29.9 %reduce-scatter.5.cloned.1.call-done = bf16[1,512,768]{2,1,0:T(8,128)(2,1)} async-done(((bf16[1,2048,768]{2,1,0:T(8,128)(2,1)}), bf16[1,512,768]{2,1,0:T(8,128)(2,1)}) %reduce-scatter.5.cloned.1.call-update) | async-done | bytes 786448 | tf_op jit(solution)/shard_map/reduce_scatter | solution.py:226
  463.6 38.7 %reduce-scatter.3.cloned.1.call-done = bf16[1,512,768]{2,1,0:T(8,128)(2,1)} async-done(((bf16[1,2048,768]{2,1,0:T(8,128)(2,1)}), bf16[1,512,768]{2,1,0:T(8,128)(2,1)}) %reduce-scatter.3.cloned.1.call-update) | async-done | bytes 786448 | tf_op jit(solution)/shard_map/reduce_scatter | solution.py:142
  502.2 3.8 fusion.93
  (261 shorter events, 78.4 us)
Async XLA Ops:
  7.2 122.1 %copy-start = (bf16[768,768]{1,0:T(8,128)(2,1)S(1)}, bf16[768,768]{1,0:T(8,128)(2,1)}, u32[]{:S(2)}) copy-start(bf16[768,768]{1,0:T(8,128)(2,1)} %param.30) | copy-start | bytes 3538948
  7.2 39.8 %copy-start.46 = (f32[768]{0:T(1024)S(1)}, f32[768]{0:T(1024)}, u32[]{:S(2)}) copy-start(f32[768]{0:T(1024)} %param.32) | copy-start | bytes 9220
  7.2 39.8 %copy-start.54 = (f32[768]{0:T(1024)S(1)}, f32[768]{0:T(1024)}, u32[]{:S(2)}) copy-start(f32[768]{0:T(1024)} %param.33) | copy-start | bytes 9220
  7.2 33.7 %all-gather.3.cloned.1.call-start = ((), (), s32[]{:S(2)}) async-start(), calls=%async_computation.2 | async-start | bytes 3932160 | tf_op jit(solution)/shard_map/all_gather | solution.py:86
  7.9 83.1 %all-gather.5.cloned.1.call-start = ((), (), s32[]{:S(2)}) async-start(), calls=%async_computation.4 | async-start | bytes 3932160 | tf_op jit(solution)/shard_map/all_gather | solution.py:87
  12.7 278.8 %all-reduce.5.cloned.1.call-start = ((), (), s32[]{:S(2)}) async-start(), calls=%async_computation.6 | async-start | bytes 811008 | tf_op jit(solution)/shard_map/psum | solution.py:244
  12.8 28.1 %copy-start.51 = (f32[8]{0:T(128)}, f32[8]{0:T(128)S(1)}, u32[]{:S(2)}) copy-start(f32[8]{0:T(128)S(1)} %multiply_power_fusion) | copy-start | bytes 100
  17.0 35.2 %copy-start.18 = (f32[2048,8]{0,1:T(8,128)}, f32[2048,8]{0,1:T(8,128)S(1)}, u32[]{:S(2)}) copy-start(f32[2048,8]{0,1:T(8,128)S(1)} %get-tuple-element.99) | copy-start | bytes 196612
  17.0 31.5 %copy-start.20 = (bf16[768,128]{1,0:T(8,128)(2,1)S(1)}, bf16[768,128]{1,0:T(8,128)(2,1)}, u32[]{:S(2)}) copy-start(bf16[768,128]{1,0:T(8,128)(2,1)} %param.28) | copy-start | bytes 589828
  50.9 10.8 %copy-start.25 = (bf16[1,2048,1,8]{1,3,2,0:T(8,128)(2,1)}, bf16[1,2048,1,8]{1,3,2,0:T(8,128)(2,1)S(1)}, u32[]{:S(2)}) copy-start(bf16[1,2048,1,8]{1,3,2,0:T(8,128)(2,1)S(1)} %get-tuple-element.91) | copy-start | bytes 98308
  50.9 10.8 %copy-start.27 = (bf16[1,2048,1,8]{1,3,2,0:T(8,128)(2,1)}, bf16[1,2048,1,8]{1,3,2,0:T(8,128)(2,1)S(1)}, u32[]{:S(2)}) copy-start(bf16[1,2048,1,8]{1,3,2,0:T(8,128)(2,1)S(1)} %get-tuple-element.92) | copy-start | bytes 98308
  50.9 10.8 %copy-start.12 = (bf16[1,2048,1,48]{1,3,2,0:T(8,128)(2,1)}, bf16[1,2048,1,48]{1,3,2,0:T(8,128)(2,1)S(1)}, u32[]{:S(2)}) copy-start(bf16[1,2048,1,48]{1,3,2,0:T(8,128)(2,1)S(1)} %slice.387) | copy-start | bytes 589828
  57.1 21.4 %copy-start.10 = (f32[512,3,1024]{2,0,1:T(8,128)}, f32[512,3,1024]{2,0,1:T(8,128)S(1)}, u32[]{:S(2)}) copy-start(f32[512,3,1024]{2,0,1:T(8,128)S(1)} %get-tuple-element.105) | copy-start | bytes 18874372
  70.4 8.1 %copy-start.16 = (bf16[1,2048,128]{1,2,0:T(8,128)(2,1)S(1)}, bf16[1,2048,128]{1,2,0:T(8,128)(2,1)}, u32[]{:S(2)}) copy-start(bf16[1,2048,128]{1,2,0:T(8,128)(2,1)} %get-tuple-element.102) | copy-start | bytes 1572868
  70.4 11.3 %slice-start = ((s8[9437184]{0:T(1024)(128)(4,1)}), s8[1048576]{0:T(1024)(128)(4,1)S(1)}, s32[]{:S(2)}) async-start(s8[9437184]{0:T(1024)(128)(4,1)} %bitcast.278), calls=%async_computation.8 | async-start | bytes 2097152
  94.1 7.4 %copy-start.8 = (f32[512,3,512]{0,2,1:T(8,128)S(1)}, f32[512,3,512]{0,2,1:T(8,128)}, u32[]{:S(2)}) copy-start(f32[512,3,512]{0,2,1:T(8,128)} %copy-done.7) | copy-start | bytes 9437188
  94.2 9.4 %slice-start.9 = ((s8[12582912]{0:T(1024)(128)(4,1)}), s8[4194304]{0:T(1024)(128)(4,1)S(1)}, s32[]{:S(2)}) async-start(s8[12582912]{0:T(1024)(128)(4,1)} %bitcast.284), calls=%async_computation.17 | async-start | bytes 8388608
  94.2 9.4 %slice-start.10 = ((s8[12582912]{0:T(1024)(128)(4,1)}), s8[4194304]{0:T(1024)(128)(4,1)S(1)}, s32[]{:S(2)}) async-start(s8[12582912]{0:T(1024)(128)(4,1)} %bitcast.284), calls=%async_computation.18 | async-start | bytes 8388608
  130.1 17.6 %copy-start.56 = (bf16[1,2048,768]{2,1,0:T(8,128)(2,1)S(1)}, bf16[1,2048,768]{2,1,0:T(8,128)(2,1)}, u32[]{:S(2)}) copy-start(bf16[1,2048,768]{2,1,0:T(8,128)(2,1)} %all-gather.5.cloned.1.call-done) | copy-start | bytes 9437188
  130.1 17.6 %copy-start.58 = (bf16[768,768]{1,0:T(8,128)(2,1)S(1)}, bf16[768,768]{1,0:T(8,128)(2,1)}, u32[]{:S(2)}) copy-start(bf16[768,768]{1,0:T(8,128)(2,1)} %param.31) | copy-start | bytes 3538948
  165.5 257.0 %all-reduce.7.cloned.1.call-start = ((), (), s32[]{:S(2)}) async-start(), calls=%async_computation.7 | async-start | bytes 5898240 | tf_op jit(solution)/shard_map/psum | solution.py:236
  179.7 282.0 %reduce-scatter.5.cloned.1.call-start = ((), (), s32[]{:S(2)}) async-start(), calls=%async_computation.5 | async-start | bytes 3932160 | tf_op jit(solution)/shard_map/reduce_scatter | solution.py:226
  180.3 321.9 %reduce-scatter.3.cloned.1.call-start = ((), (), s32[]{:S(2)}) async-start(), calls=%async_computation.3 | async-start | bytes 3932160 | tf_op jit(solution)/shard_map/reduce_scatter | solution.py:142
  188.3 314.0 %copy-start.11 = (bf16[1,512,768]{2,1,0:T(8,128)(2,1)S(1)}, bf16[1,512,768]{2,1,0:T(8,128)(2,1)}, u32[]{:S(2)}) copy-start(bf16[1,512,768]{2,1,0:T(8,128)(2,1)} %param.24) | copy-start | bytes 2359300
  (61 other events, 238.7 us)
Sparse Core Ops, SparseCore 0:
  9.6 31.2 all-gather.2
  43.0 28.6 all-gather.4
  165.6 125.9 all-reduce.4
  296.6 125.8 all-reduce.6
  424.8 36.7 reduce-scatter.4
  464.2 37.9 reduce-scatter.2

commit v2 on v0

v2 whole, which is shorter than its diff:
```python
import functools

import jax
import jax.numpy as jnp
import numpy as np
from jax import lax
from jax.experimental import pallas as pl
from jax.experimental.pallas import tpu as pltpu
from jax.sharding import PartitionSpec as P

HD = 64
ROT = 16
HALF = ROT // 2
TILE = 256
LANES = 128
MESH = pl.DeviceIdType.MESH
BF = jnp.bfloat16
F32 = jnp.float32


def mm(left, right):
    return jnp.dot(left, right, preferred_element_type=F32)


def mm_t(left, right):
    return lax.dot_general(left, right, (((1,), (1,)), ((), ())), preferred_element_type=F32)


def turn(values, cosine, sine):
    front, back = values[:HALF], values[HALF:ROT]
    return jnp.concatenate(
        [front * cosine - back * sine, back * cosine + front * sine, values[ROT:]], axis=0
    )


class Plan:
    def __init__(self, dp):
        self.bits = dp.bit_length() - 1
        self.extra = list(range(3, self.bits))
        self.stages = 6 + len(self.extra)
        self.orders = ((0, 1, 2), (1, 0, 2))


class Bundle:
    def __init__(self, plan, d, t, part, landed, swapped, total, send, recv):
        self.plan, self.d, self.t = plan, d, t
        self.part, self.landed, self.swapped, self.total = part, landed, swapped, total
        self.send, self.recv = send, recv
        self.rows = part.shape[1]

    def bit(self, position):
        return (self.d // (2**position)) % 2

    def partner(self, position):
        return self.d + (1 - 2 * self.bit(position)) * (2**position)

    def span(self, kind, depth):
        start = 0
        for level in range(depth):
            start = start + self.bit(self.plan.orders[kind][level]) * (self.rows >> (level + 1))
        return pl.multiple_of(start, 16), self.rows >> depth

    def copy(self, unit, kind, stage):
        order, extra = self.plan.orders[kind], self.plan.extra
        if stage < 3:
            start, size = self.span(kind, stage)
            position = order[stage]
            half = size // 2
            other = pl.multiple_of(start + (1 - self.bit(position)) * half, 16)
            source = self.part.at[unit, pl.ds(other, half)]
            target = self.landed.at[unit, pl.ds(self.rows - size, half)]
        elif stage < 3 + len(extra):
            start, size = self.span(kind, 3)
            position = extra[stage - 3]
            source = self.part.at[unit, pl.ds(start, size)]
            target = self.swapped.at[unit, stage - 3]
        else:
            depth = self.plan.stages - stage
            start, size = self.span(kind, depth)
            position = order[depth - 1]
            source = self.total.at[unit, pl.ds(start, size)]
            target = source
        return pltpu.make_async_remote_copy(
            src_ref=source,
            dst_ref=target,
            send_sem=self.send.at[unit, stage],
            recv_sem=self.recv.at[unit, stage],
            device_id=(self.partner(position), self.t),
            device_id_type=MESH,
        )

    def start(self, unit, kind, stage):
        self.copy(unit, kind, stage).start()

    def finish(self, unit, kind, stage, publish=True):
        self.copy(unit, kind, stage).wait()
        last = 2 + len(self.plan.extra)
        if stage <= last:
            if stage < 3:
                start, size = self.span(kind, stage + 1)
                arrived = self.landed[unit, pl.ds(self.rows - 2 * size, size)]
            else:
                start, size = self.span(kind, 3)
                arrived = self.swapped[unit, stage - 3]
            mine = self.part[unit, pl.ds(start, size)]
            summed = (mine.astype(F32) + arrived.astype(F32)).astype(BF)
            if stage == last and publish:
                self.total[unit, pl.ds(start, size)] = summed
            else:
                self.part[unit, pl.ds(start, size)] = summed


def block_kernel(
    plan,
    tags_ref,
    tag_weight_ref,
    tok_ref,
    cot_ref,
    query_ref,
    keyval_ref,
    output_ref,
    up_ref,
    down_ref,
    norms_ref,
    table_ref,
    block_out_ref,
    grad_tokens_ref,
    total_ref,
    total_small_ref,
    x_all,
    gr_all,
    n1_all,
    br_all,
    g_all,
    up_t,
    down_t,
    qkv_t,
    qkv_w,
    out_t,
    q_t,
    k_t,
    k_r,
    v_t,
    v_r,
    do_t,
    gq_all,
    norms_c,
    bias_acc,
    sum_out,
    sum_qkv,
    score,
    prob,
    acc,
    d_key,
    d_value,
    part,
    landed,
    swapped,
    part_small,
    landed_small,
    swapped_small,
    tp_land,
    tp_land_small,
    pre,
    from_sib,
    from_x,
    ag_send,
    ag_recv,
    rs_send,
    rs_recv,
    rs_send_x,
    rs_recv_x,
    dp_send,
    dp_recv,
    dp_send_small,
    dp_recv_small,
    tp_send,
    tp_recv,
):
    d, t = lax.axis_index("dp"), lax.axis_index("tp")
    chip, core = t // 2, t % 2
    sib = t + 1 - 2 * core
    across = (t + 2) % 4
    diag = (sib + 2) % 4
    width = tok_ref.shape[1]
    hidden = up_ref.shape[1]
    q_cols = query_ref.shape[1]
    heads = q_cols // HD
    own_blocks = tok_ref.shape[0] // TILE
    blocks = 4 * own_blocks
    half_width = width // 2
    tall = width // TILE

    big = Bundle(plan, d, t, part, landed, swapped, total_ref, dp_send, dp_recv)
    small = Bundle(
        plan, d, t, part_small, landed_small, swapped_small, total_small_ref, dp_send_small, dp_recv_small
    )

    barrier = pltpu.get_barrier_semaphore()
    peers = [(d, sib), (d, across), (d, diag)] + [(big.partner(b), t) for b in range(plan.bits)]
    for peer in peers:
        pl.semaphore_signal(barrier, inc=1, device_id=peer, device_id_type=MESH)
    pl.semaphore_wait(barrier, len(peers))

    row_weight = tag_weight_ref[tags_ref[0]]

    sets = (x_all, gr_all)

    def gather_copy(kind, piece, owner, route):
        place = owner * own_blocks + piece
        target = {0: sib, 1: across, 2: sib}[route]
        return pltpu.make_async_remote_copy(
            src_ref=sets[kind].at[place],
            dst_ref=sets[kind].at[place],
            send_sem=ag_send.at[kind, piece, route],
            recv_sem=ag_recv.at[kind, piece, route],
            device_id=(d, target),
            device_id_type=MESH,
        )

    for piece in range(own_blocks):
        rows = slice(piece * TILE, (piece + 1) * TILE)
        x_all[t * own_blocks + piece] = tok_ref[rows, :].T
        gather_copy(0, piece, t, 1).start()
        gather_copy(0, piece, t, 0).start()
        gr_all[t * own_blocks + piece] = (cot_ref[rows, :].astype(F32) * row_weight).astype(BF).T
        gather_copy(1, piece, t, 1).start()
        gather_copy(1, piece, t, 0).start()

    up_t[...] = up_ref[...].T
    down_t[...] = down_ref[...].T
    qkv_t[:q_cols] = query_ref[...].T
    qkv_t[q_cols:] = keyval_ref[...].T
    qkv_w[...] = qkv_t[...].T
    out_t[...] = output_ref[...].T
    norms_c[...] = norms_ref[...].T
    score[...] = jnp.zeros_like(score)
    bias_acc[...] = jnp.zeros_like(bias_acc)
    sum_out[...] = jnp.zeros_like(sum_out)
    sum_qkv[...] = jnp.zeros_like(sum_qkv)
    d_key[...] = jnp.zeros_like(d_key)
    d_value[...] = jnp.zeros_like(d_value)

    def standardize(place):
        x = x_all[place].astype(F32)
        mean = jnp.sum(x, axis=0, keepdims=True) * (1.0 / width)
        centred = x - mean
        variance = jnp.sum(centred * centred, axis=0, keepdims=True) * (1.0 / width)
        inverse = lax.rsqrt(variance + 1e-05)
        return centred * inverse, inverse

    def feed_forward(step, carry):
        late = step // 4
        owner = (1 - late) * (t + (sib - t) * ((step // 2) % 2)) + late * (
            across + (diag - across) * (step % 2)
        )
        piece = (1 - late) * (step % 2) + late * ((step // 2) % 2)
        place = owner * own_blocks + piece

        @pl.when((step == 2) | (step == 3))
        def _():
            for kind in range(2):
                gather_copy(kind, piece, sib, 0).wait_recv()

        @pl.when((step == 4) | (step == 6))
        def _():
            for kind in range(2):
                gather_copy(kind, piece, across, 1).wait_recv()
                gather_copy(kind, piece, across, 2).start()

        @pl.when((step == 5) | (step == 7))
        def _():
            for kind in range(2):
                gather_copy(kind, piece, diag, 2).wait_recv()

        normal, _ = standardize(place)
        n1 = (normal * norms_c[:, 0:1] + norms_c[:, 1:2]).astype(BF)
        n2 = (normal * norms_c[:, 2:3] + norms_c[:, 3:4]).astype(BF)
        n1_all[place] = n1
        gr = gr_all[place]
        qkv = mm(qkv_t[...], n1)
        lanes = pl.ds(pl.multiple_of(place * TILE, TILE), TILE)
        cosine, sine = table_ref[:HALF, lanes], table_ref[HALF:, lanes]
        grad_context = mm(output_ref[...], gr)
        for head in range(heads):
            turned = turn(qkv[head * HD : (head + 1) * HD], cosine, sine) * (HD**-0.5)
            q_t[place, :, head * TILE : (head + 1) * TILE] = turned.astype(BF)
            do_t[place, :, head * TILE : (head + 1) * TILE] = grad_context[
                head * HD : (head + 1) * HD
            ].astype(BF)
        key = turn(qkv[q_cols : q_cols + HD], cosine, sine)
        value = qkv[q_cols + HD :]
        k_t[place] = key.astype(BF)
        k_r[place] = key.T.astype(BF)
        v_t[place, :HD] = value.astype(BF)
        v_t[place, HD:] = jnp.ones((v_t.shape[1] - HD, TILE), BF)
        v_r[place] = value.T.astype(BF)

        pre_act = mm(up_t[...], n2)
        cdf = 0.5 + 0.5 * lax.erf(pre_act * 0.7071067811865476)
        density = jnp.exp(-0.5 * pre_act * pre_act) * 0.3989422804014327
        middle = (pre_act * cdf).astype(BF)
        slope = cdf + pre_act * density
        br_all[place] = mm(down_t[...], middle).astype(BF)
        grad_hidden = (mm(down_ref[...], gr) * slope).astype(BF)
        up_two = mm(up_ref[...], grad_hidden)
        bias_acc[...] += up_two[:, :LANES] + up_two[:, LANES:]
        g_all[place] = (up_two * norms_c[:, 2:3]).astype(BF)
        score[:tall] += mm_t(middle, gr).reshape(tall, TILE, width)
        score[tall : 2 * tall] += mm_t(n2, grad_hidden).reshape(tall, TILE, hidden)
        return carry

    lax.fori_loop(0, blocks, feed_forward, 0)

    for piece in range(own_blocks):
        for kind in range(2):
            gather_copy(kind, piece, t, 0).wait_send()
            gather_copy(kind, piece, t, 1).wait_send()
            gather_copy(kind, piece, across, 2).wait_send()

    slices = width // LANES
    for index in range(slices):
        cols = slice(index * LANES, (index + 1) * LANES)
        part[2 * index] = score[:tall, :, cols].reshape(hidden, LANES).astype(BF)
        part[2 * index + 1] = score[tall : 2 * tall, :, cols].reshape(width, LANES).astype(BF)
    for index in range(tall):
        rows = slice(index * TILE, (index + 1) * TILE)
        product = jnp.sum(up_ref[rows, :].astype(F32) * score[tall + index], axis=1, keepdims=True)
        norms_c[rows, 4:5] = product
    norms_c[:, 5:6] = jnp.sum(bias_acc[...], axis=1, keepdims=True)
    bias_acc[...] = jnp.zeros_like(bias_acc)

    outs = (br_all, g_all)

    def block_of(step):
        return (blocks - 1) - step // 2 - (blocks // 2) * (step % 2)

    def pre_copy(kind, step, block):
        rows = pl.ds(pl.multiple_of((1 - core) * half_width, 16), half_width)
        return pltpu.make_async_remote_copy(
            src_ref=outs[kind].at[block, rows],
            dst_ref=pre.at[kind, step // 2],
            send_sem=rs_send.at[kind, step],
            recv_sem=rs_recv.at[kind, step],
            device_id=(d, sib),
            device_id_type=MESH,
        )

    def sib_copy(kind, step, block):
        return pltpu.make_async_remote_copy(
            src_ref=outs[kind].at[block],
            dst_ref=from_sib.at[kind, block % own_blocks],
            send_sem=rs_send.at[kind, step],
            recv_sem=rs_recv.at[kind, step],
            device_id=(d, sib),
            device_id_type=MESH,
        )

    def x_copy(kind, block, sender_core, owner):
        rows = pl.ds(pl.multiple_of(sender_core * half_width, 16), half_width)
        return pltpu.make_async_remote_copy(
            src_ref=outs[kind].at[block, rows],
            dst_ref=from_x.at[kind, block % own_blocks, rows],
            send_sem=rs_send_x.at[kind, block],
            recv_sem=rs_recv_x.at[kind, block % own_blocks, sender_core],
            device_id=(d, owner),
            device_id_type=MESH,
        )

    def scatter_first(kind, step):
        block = block_of(step)
        owner = block // own_blocks

        @pl.when(owner // 2 != chip)
        def _():
            pre_copy(kind, step, block).start()

        @pl.when((owner // 2 == chip) & (owner != t))
        def _():
            sib_copy(kind, step, block).start()

    def scatter_second(kind, step):
        block = block_of(step)
        owner = block // own_blocks

        @pl.when(owner // 2 != chip)
        def _():
            pre_copy(kind, step, block).wait()
            rows = pl.ds(pl.multiple_of(core * half_width, 16), half_width)
            mine = outs[kind][block, rows].astype(F32)
            outs[kind][block, rows] = (mine + pre[kind, step // 2].astype(F32)).astype(BF)
            x_copy(kind, block, core, owner).start()

        @pl.when((owner // 2 == chip) & (owner != t))
        def _():
            sib_copy(kind, step, block).wait_send()

    def scatter_sent(kind, step):
        block = block_of(step)
        owner = block // own_blocks

        @pl.when(owner // 2 != chip)
        def _():
            x_copy(kind, block, core, owner).wait_send()

    def scatter_arrived(kind, piece):
        block = t * own_blocks + piece
        step = 2 * ((blocks - 1 - block) % (blocks // 2)) + 1 - block // (blocks // 2)
        sib_copy(kind, step, block).wait_recv()
        for sender_core in range(2):
            x_copy(kind, block, sender_core, t).wait_recv()
        return (
            outs[kind][block].astype(F32)
            + from_sib[kind, piece].astype(F32)
            + from_x[kind, piece].astype(F32)
        )

    pairs = slices

    def slot(index):
        for stage in range(plan.stages, -1, -1):
            pair = index - stage

            @pl.when((pair >= 0) & (pair < pairs))
            def _():
                if stage > 0:
                    for kind in range(2):
                        big.finish(2 * pair + kind, kind, stage - 1)
                if stage < plan.stages:
                    for kind in range(2):
                        big.start(2 * pair + kind, kind, stage)

    def attend(step, carry):
        slot(step)
        block = block_of(step)
        queries = q_t[block]
        wide = heads * TILE

        def scores(j, top):
            tile = mm(k_r[j], queries)
            score[j] = tile
            return jnp.maximum(top, jnp.max(tile.reshape(TILE // 8, 8, wide), axis=0))

        top = lax.fori_loop(0, block, scores, jnp.full((8, wide), -1e30, F32))
        tile = mm(k_r[block], queries)
        past = lax.broadcasted_iota(jnp.int32, (TILE, wide), 0)
        now = lax.broadcasted_iota(jnp.int32, (TILE, wide), 1) % TILE
        tile = jnp.where(past <= now, tile, -1e30)
        score[block] = tile
        top = jnp.maximum(top, jnp.max(tile.reshape(TILE // 8, 8, wide), axis=0))
        top = jnp.max(top, axis=0, keepdims=True)

        acc[...] = jnp.zeros_like(acc)

        def weigh(j, carry):
            weights = jnp.exp(score[j] - top).astype(BF)
            prob[j] = weights
            acc[...] += mm(v_t[j], weights)
            return carry

        lax.fori_loop(0, block + 1, weigh, 0)
        inverse = 1.0 / acc[HD : HD + 1]
        context = acc[:HD] * inverse
        grad = (do_t[block].astype(F32) * inverse).astype(BF)
        delta = jnp.sum(grad.astype(F32) * context, axis=0, keepdims=True)
        grad_rows = grad.astype(F32).T.astype(BF)
        query_rows = queries.astype(F32).T.astype(BF)
        acc[:HD] = jnp.zeros((HD, wide), F32)

        def back(j, carry):
            weights = prob[j]
            grad_scores = (
                weights.astype(F32) * (mm(v_r[j], grad) - delta)
            ).astype(BF)
            acc[:HD] += mm(k_t[j], grad_scores)
            d_key[j] += mm(grad_scores, query_rows)
            d_value[j] += mm(weights, grad_rows)
            return carry

        lax.fori_loop(0, block + 1, back, 0)
        lanes = pl.ds(pl.multiple_of(block * TILE, TILE), TILE)
        cosine, sine = table_ref[:HALF, lanes], table_ref[HALF:, lanes]
        for head in range(heads):
            cols = slice(head * TILE, (head + 1) * TILE)
            turned = turn(acc[:HD, cols], cosine, -sine) * (HD**-0.5)
            gq_all[block, head * HD : (head + 1) * HD] = turned.astype(BF)
        context = jnp.concatenate(
            [context[:, h * TILE : (h + 1) * TILE] for h in range(heads)], axis=0
        ).astype(BF)
        br_all[block] = (mm(out_t[...], context) + br_all[block].astype(F32)).astype(BF)
        sum_out[...] += mm_t(context, gr_all[block])
        scatter_first(0, step)

        @pl.when(step > 0)
        def _():
            scatter_second(0, step - 1)

        return carry

    lax.fori_loop(0, blocks, attend, 0)
    scatter_second(0, blocks - 1)

    def project(step, carry):
        @pl.when(step % 2 == 0)
        def _():
            slot(blocks + step // 2)

        block = block_of(step)
        lanes = pl.ds(pl.multiple_of(block * TILE, TILE), TILE)
        cosine, sine = table_ref[:HALF, lanes], table_ref[HALF:, lanes]
        gq_all[block, q_cols : q_cols + HD] = turn(d_key[block].T, cosine, -sine).astype(BF)
        gq_all[block, q_cols + HD :] = d_value[block].T.astype(BF)
        grads = gq_all[block]
        up_one = mm(qkv_w[...], grads)
        bias_acc[...] += up_one[:, :LANES] + up_one[:, LANES:]
        g_all[block] = (g_all[block].astype(F32) + up_one * norms_c[:, 0:1]).astype(BF)
        sum_qkv[...] += mm_t(grads, n1_all[block])
        scatter_first(1, step)

        @pl.when(step > 0)
        def _():
            scatter_second(1, step - 1)

        return carry

    lax.fori_loop(0, blocks, project, 0)
    scatter_second(1, blocks - 1)
    for index in range(blocks + blocks // 2, pairs + plan.stages):
        slot(index)

    base = 2 * pairs
    for index in range(slices):
        cols = slice(index * LANES, (index + 1) * LANES)
        for which, source in ((0, sum_out[:, cols]), (1, sum_qkv[:q_cols, cols])):
            row = (2 * index + which) * q_cols
            part[base + row // width, row % width : row % width + q_cols] = source.astype(BF)
    grad_keyval = sum_qkv[q_cols:].T
    part[base + 3] = grad_keyval.astype(BF)
    shift_one = jnp.sum(bias_acc[...], axis=1, keepdims=True)
    shift_two = norms_c[:, 5:6]
    product_one = jnp.sum(qkv_t[...].astype(F32) * sum_qkv[...], axis=0, keepdims=True)
    product_one = jnp.broadcast_to(product_one, (8, width)).T[:, :1]
    gain_one = (product_one - norms_c[:, 1:2] * shift_one) / norms_c[:, 0:1]
    gain_two = (norms_c[:, 4:5] - norms_c[:, 3:4] * shift_two) / norms_c[:, 2:3]
    lane = lax.broadcasted_iota(jnp.int32, (width, 8), 1)
    columns = jnp.where(
        lane == 0, gain_one, jnp.where(lane == 1, shift_one, jnp.where(lane == 2, gain_two, shift_two))
    )
    rows = columns.T
    part_small[0] = jnp.zeros(part_small.shape[1:], BF)
    for index in range(slices):
        part_small[0, 16 * index : 16 * index + 8] = rows[
            :, index * LANES : (index + 1) * LANES
        ].astype(BF)

    ends = [(big, base + u, u % 2) for u in range(4)] + [(small, 0, 0)]
    shared = [False, False, False, True, True]
    middle_stage = 2 + len(plan.extra)
    for bundle, unit, kind in ends:
        bundle.start(unit, kind, 0)
    for stage in range(middle_stage + 1):
        for (bundle, unit, kind), wide in zip(ends, shared):
            bundle.finish(unit, kind, stage, publish=not wide)
            if stage < middle_stage or not wide:
                bundle.start(unit, kind, stage + 1)

    lands = (tp_land, tp_land_small)
    offsets = []
    for index, (bundle, unit, kind) in enumerate(ends[3:]):
        start, size = bundle.span(kind, 3)
        offsets.append((start, size))
        lands[index][t] = bundle.part[unit, pl.ds(start, size)]

    def tp_copy(index, sender, hop):
        return pltpu.make_async_remote_copy(
            src_ref=lands[index].at[sender],
            dst_ref=lands[index].at[sender],
            send_sem=tp_send.at[index, hop],
            recv_sem=tp_recv.at[index, hop],
            device_id=(d, (t + hop + 1) % 4),
            device_id_type=MESH,
        )

    for index in range(2):
        for hop in range(3):
            tp_copy(index, t, hop).start()
    for index, (bundle, unit, kind) in enumerate(ends[3:]):
        for hop in range(3):
            tp_copy(index, (t + 3 - hop) % 4, hop).wait_recv()
        start, size = offsets[index]
        land = lands[index]
        summed = land[0].astype(F32) + land[1].astype(F32) + land[2].astype(F32) + land[3].astype(F32)
        bundle.total[unit, pl.ds(start, size)] = summed.astype(BF)
        bundle.start(unit, kind, middle_stage + 1)
    for index in range(2):
        for hop in range(3):
            tp_copy(index, t, hop).wait_send()
    for stage in range(middle_stage + 1, plan.stages):
        for bundle, unit, kind in ends:
            bundle.finish(unit, kind, stage)
            if stage + 1 < plan.stages:
                bundle.start(unit, kind, stage + 1)

    for piece in range(own_blocks):
        place = t * own_blocks + piece
        cols = slice(piece * TILE, (piece + 1) * TILE)
        branch = scatter_arrived(0, piece)
        block_out_ref[:, cols] = (x_all[place].astype(F32) + branch).astype(BF)
        scaled = scatter_arrived(1, piece)
        normal, inverse = standardize(place)
        mean_one = jnp.sum(scaled, axis=0, keepdims=True) * (1.0 / width)
        mean_two = jnp.sum(scaled * normal, axis=0, keepdims=True) * (1.0 / width)
        grad_tokens_ref[:, cols] = (
            gr_all[place].astype(F32) + inverse * (scaled - mean_one - normal * mean_two)
        ).astype(BF)

    def drain(step, carry):
        for kind in range(2):
            scatter_sent(kind, step)
        return carry

    lax.fori_loop(0, blocks, drain, 0)


def shards(
    dp,
    tokens,
    cotangent,
    tags,
    tag_weight,
    query_weight,
    key_value_weight,
    output_weight,
    up_weight,
    down_weight,
    norm_gain_one,
    norm_bias_one,
    norm_gain_two,
    norm_bias_two,
):
    plan = Plan(dp)
    _, own_len, width = tokens.shape
    full_len = 4 * own_len
    q_cols, kv_cols, hidden = query_weight.shape[1], key_value_weight.shape[1], up_weight.shape[1]
    heads = q_cols // HD
    wide = heads * TILE
    blocks, own_blocks = full_len // TILE, own_len // TILE
    frequencies = (10000.0 ** (-np.arange(0, ROT, 2, dtype=np.float32) / ROT)).astype(np.float32)
    angles = frequencies[:, None] * np.arange(full_len, dtype=np.float32)[None, :]
    table = np.concatenate([np.cos(angles), np.sin(angles)], axis=0).astype(np.float32)
    norms = jnp.stack([norm_gain_one, norm_bias_one, norm_gain_two, norm_bias_two] * 2)

    slices = width // LANES
    units = 2 * slices + 4
    small_rows = LANES
    extra = max(1, len(plan.extra))
    vmem = lambda *shape, kind=BF: pltpu.VMEM(shape, kind)
    dma = lambda *shape: pltpu.SemaphoreType.DMA(shape)
    scratch = [
        vmem(blocks, width, TILE),
        vmem(blocks, width, TILE),
        vmem(blocks, width, TILE),
        vmem(blocks, width, TILE),
        vmem(blocks, width, TILE),
        vmem(hidden, width),
        vmem(width, hidden),
        vmem(q_cols + kv_cols, width),
        vmem(width, q_cols + kv_cols),
        vmem(width, q_cols),
        vmem(blocks, HD, wide),
        vmem(blocks, HD, TILE),
        vmem(blocks, TILE, HD),
        vmem(blocks, HD + 16, TILE),
        vmem(blocks, TILE, HD),
        vmem(blocks, HD, wide),
        vmem(blocks, q_cols + kv_cols, TILE),
        vmem(width, 8, kind=F32),
        vmem(width, LANES, kind=F32),
        vmem(q_cols, width, kind=F32),
        vmem(q_cols + kv_cols, width, kind=F32),
        vmem(blocks, TILE, wide, kind=F32),
        vmem(blocks, TILE, wide),
        vmem(HD + 16, wide, kind=F32),
        vmem(blocks, TILE, HD, kind=F32),
        vmem(blocks, TILE, HD, kind=F32),
        vmem(units, width, LANES),
        vmem(units, width - width // 8, LANES),
        vmem(units, extra, width // 8, LANES),
        vmem(1, small_rows, LANES),
        vmem(1, small_rows - small_rows // 8, LANES),
        vmem(1, extra, small_rows // 8, LANES),
        vmem(4, width // 8, LANES),
        vmem(4, small_rows // 8, LANES),
        vmem(2, blocks // 2, width // 2, TILE),
        vmem(2, own_blocks, width, TILE),
        vmem(2, own_blocks, width, TILE),
        dma(2, own_blocks, 3),
        dma(2, own_blocks, 3),
        dma(2, blocks),
        dma(2, blocks),
        dma(2, blocks),
        dma(2, own_blocks, 2),
        dma(units, plan.stages),
        dma(units, plan.stages),
        dma(1, plan.stages),
        dma(1, plan.stages),
        dma(2, 3),
        dma(2, 3),
    ]
    in_vmem = pl.BlockSpec(memory_space=pltpu.VMEM)
    in_smem = pl.BlockSpec(memory_space=pltpu.SMEM)
    block_out, grad_tokens, total, total_small = pl.pallas_call(
        functools.partial(block_kernel, plan),
        out_shape=(
            jax.ShapeDtypeStruct((width, own_len), BF),
            jax.ShapeDtypeStruct((width, own_len), BF),
            jax.ShapeDtypeStruct((units, width, LANES), BF),
            jax.ShapeDtypeStruct((1, small_rows, LANES), BF),
        ),
        in_specs=[in_smem] * 2 + [in_vmem] * 9,
        out_specs=(in_vmem,) * 4,
        scratch_shapes=scratch,
        compiler_params=pltpu.CompilerParams(
            collective_id=0, has_side_effects=True, vmem_limit_bytes=63 << 20
        ),
    )(
        tags,
        tag_weight,
        tokens[0],
        cotangent[0],
        query_weight,
        key_value_weight,
        output_weight,
        up_weight,
        down_weight,
        norms,
        jnp.asarray(table),
    )
    split = total[: 2 * slices].reshape(slices, 2, width, LANES).transpose(1, 2, 0, 3)
    grad_downward, grad_upward = split.reshape(2, width, width).astype(F32)
    ends = total[2 * slices : 2 * slices + 3].reshape(slices, 2, q_cols, LANES)
    grad_output = ends[:, 0].transpose(1, 0, 2).reshape(q_cols, width).astype(F32)
    grad_query = ends[:, 1].transpose(0, 2, 1).reshape(width, q_cols).astype(F32)
    grad_keyval = total[2 * slices + 3].astype(F32)
    rows = total_small[0, : 16 * slices].reshape(slices, 16, LANES)[:, :4]
    rows = rows.transpose(1, 0, 2).reshape(4, width).astype(F32)
    return (
        block_out.T[None],
        grad_tokens.T[None],
        grad_query,
        grad_keyval,
        grad_output,
        grad_upward,
        grad_downward,
        rows[0],
        rows[1],
        rows[2],
        rows[3],
    )


def solution(mesh):
    rows = P("dp", "tp", None)
    columns, depth, whole = P(None, "tp"), P("tp", None), P()
    in_specs = (rows, rows, P("dp"), whole, columns, whole, depth, columns, depth) + (whole,) * 4
    out_specs = (rows, rows, columns, whole, depth, columns, depth) + (whole,) * 4
    return jax.shard_map(
        functools.partial(shards, mesh.shape["dp"]),
        mesh=mesh,
        in_specs=in_specs,
        out_specs=out_specs,
        check_vma=False,
    )
```

time: 640 us -> 195 us (0.30)
  waiting for transfers between devices: 392 us -> 0 us
  Pallas kernels: 0 us -> 163 us
  matrix products: 132 us -> 0 us
  blocking collectives: 40.1 us -> 0 us
  other arithmetic: 33.5 us -> 2.07 us
  between operations: 16.1 us -> 1.34 us
  local copies, waits for them, and re-layouts: 19.8 us -> 27.5 us
    psum x2 -> x0, waiting for transfers between devices: 330 us -> none  [the longest x1 207 us: shards(): lax.psum((grad_query, grad_output, grad_upward, grad_downward), 'dp')]
    pallas_call x0 -> x1, Pallas kernels: none -> 163 us  [shards(): pl.pallas_call(functools.partial(block_kernel, plan), out_shape=(jax.Shap...]
    dot_general x39 -> x0, matrix products: 132 us -> none  [the longest x5 19.8 us: against(): lax.dot_general(left, weight, (((2,), (1,)), ((), ())), preferred_element...]
    psum x1 -> x0, blocking collectives: 40.1 us -> none  [shards(): lax.psum((grad_keyval, grad_gain_one, grad_bias_one, grad_gain_two, grad_...]
    reduce_scatter x4 -> x0, waiting for transfers between devices: 37.9 us -> none  [the longest x1 37.9 us: shards(): lax.psum_scatter(norm_part_one.astype(jnp.bfloat16), 'tp', scatter_dimens...]
    all_gather x3 -> x0, waiting for transfers between devices: 23.5 us -> none  [the longest x1 23.4 us: shards(): lax.all_gather(low_one, 'tp', axis=1, tiled=True)]
    reduce_sum x7 -> x0, other arithmetic: 14.2 us -> none  [the longest x4 10.6 us: shards(): row_total = jnp.sum(weights, axis=-1, keepdims=True)]
    another operation x0 -> x6, local copies, waits for them, and re-layouts: none -> 7.63 us  [the longest x1 4.22 us: shards(): grad_downward, grad_upward = split.reshape(2, width, width).astype(F32)]
  transfers between devices with their start and end apart: 9 -> 0, of which waited for: 4 -> 0; matrix products, arithmetic and copies ran while one was open for 25% -> 0% of each run, Pallas kernels for 0% -> 0%
where the time goes in v2:
time: 195 us; the launch traced here: 194 us
  Pallas kernels  163 us (84%)
  local copies, waits for them, and re-layouts  27.5 us (14%)
  other arithmetic  2.07 us (1%)
    pallas_call x1, Pallas kernels, shards(): pl.pallas_call(functools.partial(block_kernel, plan), out_shape=(jax.Shap...  163 us
    unnamed x9, local copies, waits for them, and re-layouts  13.3 us
    another operation x1, local copies, waits for them, and re-layouts, shards(): grad_downward, grad_upward = split.reshape(2, width, width).astype(F32)  4.22 us

profile of v2, /device:TPU:0, one launch (start us, length us, event | category | flops | bytes accessed | tf_op | source)
XLA Modules:
  0.0 194.1 jit_solution(17418424053861687649)
XLA Ops:
  1.3 0.7 stack.19
  2.0 0.7 stack.20
  2.7 0.7 stack.21
  3.4 0.7 stack.22
  4.0 0.6 stack.23.norms_ref
  4.7 1.9 copy.32.query_ref
  6.6 163.2 %shard_map.221 = (bf16[768,512]{1,0:T(8,128)(2,1)}, bf16[768,512]{1,0:T(8,128)(2,1)}, bf16[16,768,128]{2,1,0:T(8,128)(2,1)}, bf16[1,128,128]{2,1,0:T(8,128)(2,1)}) custom-call(s32[1]{0:T(128)S(6)} %copy.54.tags_ref, f32[8]{0:T(128)} %tag_weight_ref.1, bf16[512,768]{1,0:T(8,128)(2,1)} %bitcast.55, bf16[512,768]{1,0:T(8,128)(2,1)} %bitcast.56, ...), custom_call_target="tpu_custom_call" | custom-call | tf_op jit(solution)/shard_map/pallas_call | solution.py:712
  169.8 0.0 copy-start
  169.8 2.3 %copy.36 = bf16[1,512,768]{2,1,0:T(8,128)(2,1)} copy(bf16[1,512,768]{1,2,0:T(8,128)(2,1)} %bitcast.54) | data formatting | bytes 1572864
  172.1 2.3 %copy.37 = bf16[1,512,768]{2,1,0:T(8,128)(2,1)} copy(bf16[1,512,768]{1,2,0:T(8,128)(2,1)} %bitcast.53) | data formatting | bytes 1572864
  174.3 0.0 copy-done
  174.4 0.6 slice_reduce_fusion
  175.0 1.7 bitcast_convert_fusion
  176.7 1.1 slice.39
  177.8 1.8 slice.43
  179.7 0.4 fusion
  180.0 0.9 copy.52
  181.0 0.9 copy.53
  181.9 3.0 %copy.35 = f32[6,2,768,128]{2,3,0,1:T(8,128)} copy(bf16[6,2,768,128]{3,2,1,0:T(8,128)(2,1)S(1)} %bitcast.47) | data formatting | bytes 7077888 | tf_op jit(solution)/shard_map/convert_element_type | solution.py:740
  184.9 4.2 %fusion.2 = (f32[1,768,6,128]{1,3,2,0:T(8,128)}, f32[1,768,6,128]{1,3,2,0:T(8,128)S(1)}) fusion(f32[2,768,6,128]{1,3,2,0:T(8,128)} %bitcast.46), kind=kLoop, calls=%fused_computation.12 | loop fusion | bytes 9437184 | tf_op jit(solution)/shard_map/unstack | solution.py:740
  189.1 3.0 %copy.39 = f32[768,768]{1,0:T(8,128)} copy(f32[768,768]{0,1:T(8,128)} %bitcast.49) | data formatting | bytes 4718592
  192.1 1.9 %copy.38 = f32[768,768]{1,0:T(8,128)} copy(f32[768,768]{0,1:T(8,128)S(1)} %bitcast.48) | data formatting | bytes 4718592
  (3 shorter events, 0.1 us)
Async XLA Ops:
  169.8 4.6 %copy-start = (bf16[1,128,128]{2,1,0:T(8,128)(2,1)S(1)}, bf16[1,128,128]{2,1,0:T(8,128)(2,1)}, u32[]{:S(2)}) copy-start(bf16[1,128,128]{2,1,0:T(8,128)(2,1)} %get-tuple-element.18) | copy-start | bytes 98308

commit v3 on v2

v3 whole, which is shorter than its diff:
```python
import functools

import jax
import jax.numpy as jnp
import numpy as np
from jax import lax
from jax.experimental import pallas as pl
from jax.experimental.pallas import tpu as pltpu
from jax.sharding import PartitionSpec as P

HD = 64
ROT = 16
HALF = ROT // 2
TILE = 256
LANES = 128
MESH = pl.DeviceIdType.MESH
BF = jnp.bfloat16
F32 = jnp.float32


def mm(left, right):
    return jnp.dot(left, right, preferred_element_type=F32)


def mm_t(left, right):
    return lax.dot_general(left, right, (((1,), (1,)), ((), ())), preferred_element_type=F32)


def turn(values, cosine, sine):
    front, back = values[:HALF], values[HALF:ROT]
    return jnp.concatenate(
        [front * cosine - back * sine, back * cosine + front * sine, values[ROT:]], axis=0
    )


class Plan:
    def __init__(self, dp):
        self.bits = dp.bit_length() - 1
        self.extra = [2**position for position in range(3, self.bits)]
        self.stages = 6 + len(self.extra)
        self.lag = [1 + 2 * stage for stage in range(self.stages - 1)]
        self.lag.append(self.lag[-1] + 4)

    def strides(self, kind):
        return (1 + kind, 2 - kind, 4)


class Bundle:
    def __init__(self, plan, d, t, part, landed, swapped, total, send, recv):
        self.plan, self.d, self.t = plan, d, t
        self.part, self.landed, self.swapped, self.total = part, landed, swapped, total
        self.send, self.recv = send, recv
        self.rows = part.shape[1]

    def bit(self, stride):
        return (self.d // stride) % 2

    def partner(self, stride):
        return self.d + (1 - 2 * self.bit(stride)) * stride

    def span(self, kind, depth):
        start = 0
        for level in range(depth):
            start = start + self.bit(self.plan.strides(kind)[level]) * (self.rows >> (level + 1))
        return pl.multiple_of(start, 16), self.rows >> depth

    def copy(self, unit, kind, stage):
        order, extra = self.plan.strides(kind), self.plan.extra
        if stage < 3:
            start, size = self.span(kind, stage)
            position = order[stage]
            half = size // 2
            other = pl.multiple_of(start + (1 - self.bit(position)) * half, 16)
            source = self.part.at[unit, pl.ds(other, half)]
            target = self.landed.at[unit, pl.ds(self.rows - size, half)]
        elif stage < 3 + len(extra):
            start, size = self.span(kind, 3)
            position = extra[stage - 3]
            source = self.part.at[unit, pl.ds(start, size)]
            target = self.swapped.at[unit, stage - 3]
        else:
            depth = self.plan.stages - stage
            start, size = self.span(kind, depth)
            position = order[depth - 1]
            source = self.total.at[unit, pl.ds(start, size)]
            target = source
        return pltpu.make_async_remote_copy(
            src_ref=source,
            dst_ref=target,
            send_sem=self.send.at[unit, stage],
            recv_sem=self.recv.at[unit, stage],
            device_id=(self.partner(position), self.t),
            device_id_type=MESH,
        )

    def start(self, unit, kind, stage):
        self.copy(unit, kind, stage).start()

    def finish(self, unit, kind, stage, publish=True):
        self.copy(unit, kind, stage).wait()
        last = 2 + len(self.plan.extra)
        if stage <= last:
            if stage < 3:
                start, size = self.span(kind, stage + 1)
                arrived = self.landed[unit, pl.ds(self.rows - 2 * size, size)]
            else:
                start, size = self.span(kind, 3)
                arrived = self.swapped[unit, stage - 3]
            mine = self.part[unit, pl.ds(start, size)]
            summed = (mine.astype(F32) + arrived.astype(F32)).astype(BF)
            if stage == last and publish:
                self.total[unit, pl.ds(start, size)] = summed
            else:
                self.part[unit, pl.ds(start, size)] = summed


def block_kernel(
    plan,
    tags_ref,
    tag_weight_ref,
    tok_ref,
    cot_ref,
    query_t_ref,
    keyval_ref,
    output_ref,
    up_ref,
    down_ref,
    gain_one_ref,
    bias_one_ref,
    gain_two_ref,
    bias_two_ref,
    table_ref,
    block_out_ref,
    grad_tokens_ref,
    total_ref,
    total_small_ref,
    x_all,
    gr_all,
    n1_all,
    br_all,
    g_all,
    up_t,
    down_t,
    qkv_t,
    qkv_w,
    out_t,
    q_t,
    k_t,
    k_r,
    v_t,
    v_r,
    do_t,
    gq_all,
    norms_c,
    norms_r,
    bias_acc,
    sum_out,
    sum_qkv,
    score,
    prob,
    acc,
    d_key,
    d_value,
    part,
    landed,
    swapped,
    part_small,
    landed_small,
    swapped_small,
    tp_land,
    tp_land_small,
    pre,
    from_sib,
    from_x,
    ag_send,
    ag_recv,
    rs_send,
    rs_recv,
    rs_send_x,
    rs_recv_x,
    dp_send,
    dp_recv,
    dp_send_small,
    dp_recv_small,
    tp_send,
    tp_recv,
):
    d, t = lax.axis_index("dp"), lax.axis_index("tp")
    chip, core = t // 2, t % 2
    sib = t + 1 - 2 * core
    across = (t + 2) % 4
    diag = (sib + 2) % 4
    width = tok_ref.shape[1]
    hidden = up_ref.shape[1]
    q_cols = query_t_ref.shape[0]
    heads = q_cols // HD
    own_blocks = tok_ref.shape[0] // TILE
    blocks = 4 * own_blocks
    half_width = width // 2
    tall = width // TILE

    big = Bundle(plan, d, t, part, landed, swapped, total_ref, dp_send, dp_recv)
    small = Bundle(
        plan, d, t, part_small, landed_small, swapped_small, total_small_ref, dp_send_small, dp_recv_small
    )

    barrier = pltpu.get_barrier_semaphore()
    peers = [(d, sib), (d, across), (d, diag)] + [(big.partner(2**b), t) for b in range(plan.bits)]
    for peer in peers:
        pl.semaphore_signal(barrier, inc=1, device_id=peer, device_id_type=MESH)
    pl.semaphore_wait(barrier, len(peers))

    row_weight = tag_weight_ref[tags_ref[0]]

    sets = (x_all, gr_all)

    def pair(ref, block):
        return jnp.concatenate([ref[2 * block], ref[2 * block + 1]], axis=1)

    def put_pair(ref, block, value):
        ref[2 * block] = value[:, :LANES]
        ref[2 * block + 1] = value[:, LANES:]

    def half_lanes(start, half):
        return pl.ds(pl.multiple_of(start + half * LANES, LANES), LANES)

    def gather_copy(kind, piece, half, owner, route):
        place = owner * own_blocks + piece
        target = {0: sib, 1: across, 2: sib}[route]
        view = sets[kind].at[2 * place + half]
        return pltpu.make_async_remote_copy(
            src_ref=view,
            dst_ref=view,
            send_sem=ag_send.at[kind, piece, half, route],
            recv_sem=ag_recv.at[kind, piece, half, route],
            device_id=(d, target),
            device_id_type=MESH,
        )

    for piece in range(own_blocks):
        rows = slice(piece * TILE, (piece + 1) * TILE)
        put_pair(x_all, t * own_blocks + piece, tok_ref[rows, :].T)
        for half in range(2):
            gather_copy(0, piece, half, t, 0).start()
        gather_copy(0, piece, 0, t, 1).start()
        weighted = (cot_ref[rows, :].astype(F32) * row_weight).astype(BF).T
        put_pair(gr_all, t * own_blocks + piece, weighted)
        for half in range(2):
            gather_copy(1, piece, half, t, 0).start()
        gather_copy(1, piece, 0, t, 1).start()
        gather_copy(0, piece, 1, t, 1).start()
        gather_copy(1, piece, 1, t, 1).start()

    up_t[...] = up_ref[...].T
    down_t[...] = down_ref[...].T
    qkv_t[:q_cols] = query_t_ref[...]
    qkv_t[q_cols:] = keyval_ref[...].T
    qkv_w[...] = qkv_t[...].T
    out_t[...] = output_ref[...].T
    for index, norm in enumerate((gain_one_ref, bias_one_ref, gain_two_ref, bias_two_ref)):
        norms_r[index : index + 1] = norm[...].reshape(1, width)
    norms_c[...] = norms_r[...].T
    score[...] = jnp.zeros_like(score)
    bias_acc[...] = jnp.zeros_like(bias_acc)
    sum_out[...] = jnp.zeros_like(sum_out)
    sum_qkv[...] = jnp.zeros_like(sum_qkv)
    d_key[...] = jnp.zeros_like(d_key)
    d_value[...] = jnp.zeros_like(d_value)

    def standardize(x):
        mean = jnp.sum(x, axis=0, keepdims=True) * (1.0 / width)
        centred = x - mean
        variance = jnp.sum(centred * centred, axis=0, keepdims=True) * (1.0 / width)
        inverse = lax.rsqrt(variance + 1e-05)
        return centred * inverse, inverse

    def feed_forward(step, carry):
        late, piece, half = step // 4, (step % 4) // 2, step % 2
        owners = (
            (1 - late) * t + late * across,
            (1 - late) * sib + late * diag,
        )
        places = [owner * own_blocks + piece for owner in owners]
        sides = [slice(0, LANES), slice(LANES, TILE)]

        @pl.when(late == 0)
        def _():
            for kind in range(2):
                gather_copy(kind, piece, half, sib, 0).wait_recv()

        @pl.when(late == 1)
        def _():
            for kind in range(2):
                gather_copy(kind, piece, half, across, 1).wait_recv()
                gather_copy(kind, piece, half, across, 2).start()
            for kind in range(2):
                gather_copy(kind, piece, half, diag, 2).wait_recv()

        def load(ref):
            return jnp.concatenate([ref[2 * place + half] for place in places], axis=1)

        def store(ref, value):
            for place, side in zip(places, sides):
                ref[2 * place + half] = value[:, side]

        normal, _ = standardize(load(x_all).astype(F32))
        n1 = (normal * norms_c[:, 0:1] + norms_c[:, 1:2]).astype(BF)
        n2 = (normal * norms_c[:, 2:3] + norms_c[:, 3:4]).astype(BF)
        store(n1_all, n1)
        gr = load(gr_all)
        qkv = mm(qkv_t[...], n1)
        lanes = [half_lanes(place * TILE, half) for place in places]
        cosine = jnp.concatenate([table_ref[:HALF, at] for at in lanes], axis=1)
        sine = jnp.concatenate([table_ref[HALF:, at] for at in lanes], axis=1)
        grad_context = mm(output_ref[...], gr)
        for head in range(heads):
            rows = slice(head * HD, (head + 1) * HD)
            turned = (turn(qkv[rows], cosine, sine) * (HD**-0.5)).astype(BF)
            grads = grad_context[rows].astype(BF)
            for place, side in zip(places, sides):
                at = slice(head * LANES, (head + 1) * LANES)
                q_t[2 * place + half, :, at] = turned[:, side]
                do_t[2 * place + half, :, at] = grads[:, side]
        key = turn(qkv[q_cols : q_cols + HD], cosine, sine)
        value = qkv[q_cols + HD :]
        for place, side, at in zip(places, sides, lanes):
            k_t[:, at] = key[:, side].astype(BF)
            v_t[:HD, at] = value[:, side].astype(BF)
            v_t[HD:, at] = jnp.ones((v_t.shape[0] - HD, LANES), BF)
            k_r[place, half_lanes(0, half), :] = key[:, side].T.astype(BF)
            v_r[place, half_lanes(0, half), :] = value[:, side].T.astype(BF)

        pre_act = mm(up_t[...], n2)
        cdf = 0.5 + 0.5 * lax.erf(pre_act * 0.7071067811865476)
        density = jnp.exp(-0.5 * pre_act * pre_act) * 0.3989422804014327
        middle = (pre_act * cdf).astype(BF)
        slope = cdf + pre_act * density
        store(br_all, mm(down_t[...], middle).astype(BF))
        grad_hidden = (mm(down_ref[...], gr) * slope).astype(BF)
        up_two = mm(up_ref[...], grad_hidden)
        bias_acc[...] += up_two[:, :LANES] + up_two[:, LANES:]
        store(g_all, (up_two * norms_c[:, 2:3]).astype(BF))
        score[:tall] += mm_t(middle, gr).reshape(tall, TILE, width)
        score[tall : 2 * tall] += mm_t(n2, grad_hidden).reshape(tall, TILE, hidden)
        return carry

    lax.fori_loop(0, blocks, feed_forward, 0)

    def gathered(index, carry):
        piece, half = index // 2, index % 2
        for kind in range(2):
            gather_copy(kind, piece, half, t, 0).wait_send()
            gather_copy(kind, piece, half, t, 1).wait_send()
            gather_copy(kind, piece, half, across, 2).wait_send()
        return carry

    lax.fori_loop(0, 2 * own_blocks, gathered, 0)

    slices = width // LANES
    for index in range(slices):
        cols = slice(index * LANES, (index + 1) * LANES)
        part[2 * index] = score[:tall, :, cols].reshape(hidden, LANES).astype(BF)
        big.start(2 * index, (2 * index) % 4 // 3, 0)
        part[2 * index + 1] = score[tall : 2 * tall, :, cols].reshape(width, LANES).astype(BF)
        big.start(2 * index + 1, (2 * index + 1) % 4 // 3, 0)
    for index in range(tall):
        rows = slice(index * TILE, (index + 1) * TILE)
        product = jnp.sum(up_ref[rows, :].astype(F32) * score[tall + index], axis=1, keepdims=True)
        norms_c[rows, 4:5] = product
    norms_c[:, 5:6] = jnp.sum(bias_acc[...], axis=1, keepdims=True)
    bias_acc[...] = jnp.zeros_like(bias_acc)

    outs = (br_all, g_all)

    def block_of(step):
        return (blocks - 1) - step // 2 - (blocks // 2) * (step % 2)

    def pre_copy(kind, step, block):
        rows = pl.ds(pl.multiple_of((1 - core) * half_width, 16), half_width)
        return pltpu.make_async_remote_copy(
            src_ref=outs[kind].at[pl.ds(2 * block, 2), rows],
            dst_ref=pre.at[kind, step // 2],
            send_sem=rs_send.at[kind, step],
            recv_sem=rs_recv.at[kind, step],
            device_id=(d, sib),
            device_id_type=MESH,
        )

    def sib_copy(kind, step, block):
        return pltpu.make_async_remote_copy(
            src_ref=outs[kind].at[pl.ds(2 * block, 2)],
            dst_ref=from_sib.at[kind, block % own_blocks],
            send_sem=rs_send.at[kind, step],
            recv_sem=rs_recv.at[kind, step],
            device_id=(d, sib),
            device_id_type=MESH,
        )

    def x_copy(kind, block, sender_core, owner):
        rows = pl.ds(pl.multiple_of(sender_core * half_width, 16), half_width)
        return pltpu.make_async_remote_copy(
            src_ref=outs[kind].at[pl.ds(2 * block, 2), rows],
            dst_ref=from_x.at[kind, block % own_blocks, :, rows],
            send_sem=rs_send_x.at[kind, block],
            recv_sem=rs_recv_x.at[kind, block % own_blocks, sender_core],
            device_id=(d, owner),
            device_id_type=MESH,
        )

    def scatter_first(kind, step):
        block = block_of(step)
        owner = block // own_blocks

        @pl.when(owner // 2 != chip)
        def _():
            pre_copy(kind, step, block).start()

        @pl.when((owner // 2 == chip) & (owner != t))
        def _():
            sib_copy(kind, step, block).start()

    def scatter_second(kind, step):
        block = block_of(step)
        owner = block // own_blocks

        @pl.when(owner // 2 != chip)
        def _():
            pre_copy(kind, step, block).wait()
            rows = pl.ds(pl.multiple_of(core * half_width, 16), half_width)
            mine = outs[kind][pl.ds(2 * block, 2), rows].astype(F32)
            outs[kind][pl.ds(2 * block, 2), rows] = (mine + pre[kind, step // 2].astype(F32)).astype(BF)
            x_copy(kind, block, core, owner).start()

        @pl.when((owner // 2 == chip) & (owner != t))
        def _():
            sib_copy(kind, step, block).wait_send()

    def scatter_sent(kind, step):
        block = block_of(step)
        owner = block // own_blocks

        @pl.when(owner // 2 != chip)
        def _():
            x_copy(kind, block, core, owner).wait_send()

    def scatter_arrived(kind, piece):
        block = t * own_blocks + piece
        step = 2 * ((blocks - 1 - block) % (blocks // 2)) + 1 - block // (blocks // 2)
        sib_copy(kind, step, block).wait_recv()
        for sender_core in range(2):
            x_copy(kind, block, sender_core, t).wait_recv()
        halves = [
            outs[kind][2 * block + half].astype(F32)
            + from_sib[kind, piece, half].astype(F32)
            + from_x[kind, piece, half].astype(F32)
            for half in range(2)
        ]
        return jnp.concatenate(halves, axis=1)

    def emit_block_out(piece):
        cols = slice(piece * TILE, (piece + 1) * TILE)
        x = pair(x_all, t * own_blocks + piece).astype(F32)
        block_out_ref[:, cols] = (x + scatter_arrived(0, piece)).astype(BF)

    def emit_grad_tokens(piece):
        place = t * own_blocks + piece
        scaled = scatter_arrived(1, piece)
        normal, inverse = standardize(pair(x_all, place).astype(F32))
        mean_one = jnp.sum(scaled, axis=0, keepdims=True) * (1.0 / width)
        mean_two = jnp.sum(scaled * normal, axis=0, keepdims=True) * (1.0 / width)
        grad_tokens_ref[:, piece * TILE : (piece + 1) * TILE] = (
            pair(gr_all, place).astype(F32) + inverse * (scaled - mean_one - normal * mean_two)
        ).astype(BF)

    base = 2 * slices

    def slot(index):
        for stage in reversed(range(plan.stages)):
            unit = index - plan.lag[stage]

            @pl.when((unit >= 0) & (unit < base))
            def _():
                kind = (unit % 4) // 3
                big.finish(unit, kind, stage)
                if stage + 1 < plan.stages:
                    big.start(unit, kind, stage + 1)

    def attend(step, carry):
        slot(3 * step)
        block = block_of(step)
        queries = jnp.concatenate([q_t[2 * block], q_t[2 * block + 1]], axis=1)
        wide = heads * TILE

        def in_pairs(count, body, start):
            carry = lax.fori_loop(0, count // 4, lambda i, c: body(4 * i, 4, c), start)
            carry = lax.fori_loop(count // 4 * 2, count // 2, lambda i, c: body(2 * i, 2, c), carry)
            return lax.fori_loop(count // 2 * 2, count, lambda i, c: body(i, 1, c), carry)

        def lanes_of(j, tiles):
            return pl.ds(pl.multiple_of(j * TILE, TILE), tiles * TILE)

        def scores(j, tiles, top):
            tile = mm(k_r[pl.ds(j, tiles)].reshape(tiles * TILE, HD), queries)
            score[pl.ds(j, tiles)] = tile.reshape(tiles, TILE, wide)
            return jnp.maximum(top, jnp.max(tile.reshape(tiles * TILE // 8, 8, wide), axis=0))

        top = in_pairs(block, scores, jnp.full((8, wide), -1e30, F32))
        tile = mm(k_r[block], queries)
        past = lax.broadcasted_iota(jnp.int32, (TILE, wide), 0)
        now = lax.broadcasted_iota(jnp.int32, (TILE, wide), 1)
        now = now // (wide // 2) * LANES + now % LANES
        tile = jnp.where(past <= now, tile, -1e30)
        score[block] = tile
        top = jnp.maximum(top, jnp.max(tile.reshape(TILE // 8, 8, wide), axis=0))
        top = jnp.max(top, axis=0, keepdims=True)

        acc[...] = jnp.zeros_like(acc)
        slot(3 * step + 1)

        def weigh(j, tiles, carry):
            weights = jnp.exp(score[pl.ds(j, tiles)] - top).astype(BF)
            prob[pl.ds(j, tiles)] = weights
            acc[...] += mm(v_t[:, lanes_of(j, tiles)], weights.reshape(tiles * TILE, wide))
            return carry

        in_pairs(block + 1, weigh, 0)
        inverse = 1.0 / acc[HD : HD + 1]
        context = acc[:HD] * inverse
        grad = (pair(do_t, block).astype(F32) * inverse).astype(BF)
        delta = jnp.sum(grad.astype(F32) * context, axis=0, keepdims=True)
        acc[:HD] = jnp.zeros((HD, wide), F32)

        slot(3 * step + 2)

        def back(j, tiles, carry):
            weights = prob[pl.ds(j, tiles)].reshape(tiles * TILE, wide)
            grad_probs = mm(v_r[pl.ds(j, tiles)].reshape(tiles * TILE, HD), grad)
            grad_scores = (weights.astype(F32) * (grad_probs - delta)).astype(BF)
            acc[:HD] += mm(k_t[:, lanes_of(j, tiles)], grad_scores)
            d_key[:, lanes_of(j, tiles)] += mm_t(queries, grad_scores)
            d_value[:, lanes_of(j, tiles)] += mm_t(grad, weights)
            return carry

        in_pairs(block + 1, back, 0)
        lanes = pl.ds(pl.multiple_of(block * TILE, TILE), TILE)
        cosine, sine = table_ref[:HALF, lanes], table_ref[HALF:, lanes]
        def of_head(value, head):
            first = value[:, head * LANES : (head + 1) * LANES]
            second = value[:, (heads + head) * LANES : (heads + head + 1) * LANES]
            return jnp.concatenate([first, second], axis=1)

        grad_queries = acc[:HD]
        for head in range(heads):
            turned = turn(of_head(grad_queries, head), cosine, -sine) * (HD**-0.5)
            gq_all[block, head * HD : (head + 1) * HD] = turned.astype(BF)
        context = jnp.concatenate([of_head(context, h) for h in range(heads)], axis=0).astype(BF)
        branch = mm(out_t[...], context) + pair(br_all, block).astype(F32)
        put_pair(br_all, block, branch.astype(BF))
        sum_out[...] += mm_t(context, pair(gr_all, block))
        sum_qkv[:q_cols] += mm_t(gq_all[block, :q_cols], pair(n1_all, block))
        scatter_first(0, step)

        @pl.when(step > 0)
        def _():
            scatter_second(0, step - 1)

        return carry

    lax.fori_loop(0, blocks, attend, 0)
    scatter_second(0, blocks - 1)

    for index in range(slices):
        cols = slice(index * LANES, (index + 1) * LANES)
        for which, source in ((0, sum_out[:, cols]), (1, sum_qkv[:q_cols, cols])):
            row = (2 * index + which) * q_cols
            part[base + row // width, row % width : row % width + q_cols] = source.astype(BF)
    first_ends = [(big, base, 0), (big, base + 1, 1), (big, base + 2, 0)]
    for bundle, unit, kind in first_ends:
        bundle.start(unit, kind, 0)

    def project(step, carry):
        slot(3 * blocks + step)
        block = block_of(step)
        lanes = pl.ds(pl.multiple_of(block * TILE, TILE), TILE)
        cosine, sine = table_ref[:HALF, lanes], table_ref[HALF:, lanes]
        gq_all[block, q_cols : q_cols + HD] = turn(d_key[:, lanes], cosine, -sine).astype(BF)
        gq_all[block, q_cols + HD :] = d_value[:, lanes].astype(BF)
        grads = gq_all[block]
        up_one = mm(qkv_w[...], grads)
        bias_acc[...] += up_one[:, :LANES] + up_one[:, LANES:]
        put_pair(g_all, block, (pair(g_all, block).astype(F32) + up_one * norms_c[:, 0:1]).astype(BF))
        sum_qkv[q_cols:] += mm_t(grads[q_cols:], pair(n1_all, block))
        scatter_first(1, step)

        @pl.when(step > 0)
        def _():
            scatter_second(1, step - 1)

        for stage, when in ((0, 4), (1, 7)):

            @pl.when(step == when)
            def _():
                for bundle, unit, kind in first_ends:
                    bundle.finish(unit, kind, stage)
                    bundle.start(unit, kind, stage + 1)

        return carry

    lax.fori_loop(0, blocks, project, 0)
    scatter_second(1, blocks - 1)
    for index in range(4 * blocks, base + plan.lag[-1]):
        slot(index)

    grad_keyval = sum_qkv[q_cols:].T
    part[base + 3] = grad_keyval.astype(BF)
    shift_one = jnp.sum(bias_acc[...], axis=1, keepdims=True)
    shift_two = norms_c[:, 5:6]
    product_one = jnp.sum(qkv_t[...].astype(F32) * sum_qkv[...], axis=0, keepdims=True)
    product_one = jnp.broadcast_to(product_one, (8, width)).T[:, :1]
    gain_one = (product_one - norms_c[:, 1:2] * shift_one) / norms_c[:, 0:1]
    gain_two = (norms_c[:, 4:5] - norms_c[:, 3:4] * shift_two) / norms_c[:, 2:3]
    lane = lax.broadcasted_iota(jnp.int32, (width, 8), 1)
    columns = jnp.where(
        lane == 0, gain_one, jnp.where(lane == 1, shift_one, jnp.where(lane == 2, gain_two, shift_two))
    )
    rows = columns.T
    part_small[0] = jnp.zeros(part_small.shape[1:], BF)
    for index in range(slices):
        part_small[0, 16 * index : 16 * index + 8] = rows[
            :, index * LANES : (index + 1) * LANES
        ].astype(BF)

    last_ends = [(big, base + 3, 1), (small, 0, 0)]
    for bundle, unit, kind in last_ends:
        bundle.start(unit, kind, 0)
    lands = (tp_land, tp_land_small)

    def tp_copy(index, sender, hop):
        return pltpu.make_async_remote_copy(
            src_ref=lands[index].at[sender],
            dst_ref=lands[index].at[sender],
            send_sem=tp_send.at[index, hop],
            recv_sem=tp_recv.at[index, hop],
            device_id=(d, (t + hop + 1) % 4),
            device_id_type=MESH,
        )

    middle_stage = 2 + len(plan.extra)
    for beat in range(plan.stages + 1):
        stage = beat + 2
        if stage < plan.stages:
            for bundle, unit, kind in first_ends:
                bundle.finish(unit, kind, stage)
                if stage + 1 < plan.stages:
                    bundle.start(unit, kind, stage + 1)
        for index, (bundle, unit, kind) in enumerate(last_ends):
            rows = pl.ds(*bundle.span(kind, 3))
            if beat < middle_stage:
                bundle.finish(unit, kind, beat)
                bundle.start(unit, kind, beat + 1)
            elif beat == middle_stage:
                bundle.finish(unit, kind, beat, publish=False)
                lands[index][t] = bundle.part[unit, rows]
                for hop in range(3):
                    tp_copy(index, t, hop).start()
            elif beat == middle_stage + 1:
                for hop in range(3):
                    tp_copy(index, (t + 3 - hop) % 4, hop).wait_recv()
                land = [lands[index][sender].astype(F32) for sender in range(4)]
                bundle.total[unit, rows] = (land[0] + land[1] + land[2] + land[3]).astype(BF)
                bundle.start(unit, kind, beat)
            else:
                bundle.finish(unit, kind, beat - 1)
                if beat < plan.stages:
                    bundle.start(unit, kind, beat)
        if beat == 0:
            for piece in range(own_blocks):
                emit_block_out(piece)
    for index in range(2):
        for hop in range(3):
            tp_copy(index, t, hop).wait_send()
    for piece in range(own_blocks):
        emit_grad_tokens(piece)

    def drain(step, carry):
        for kind in range(2):
            scatter_sent(kind, step)
        return carry

    lax.fori_loop(0, blocks, drain, 0)


def finish_kernel(
    block_out_t,
    grad_tokens_t,
    split,
    ends,
    keyval,
    small,
    block_out_ref,
    grad_tokens_ref,
    grad_query_ref,
    grad_keyval_ref,
    grad_output_ref,
    grad_up_ref,
    grad_down_ref,
    *vector_refs,
):
    block_out_ref[...] = block_out_t[...].T
    grad_tokens_ref[...] = grad_tokens_t[...].T
    grad_output_ref[...] = ends[0].astype(F32)
    grad_query_ref[...] = ends[1].astype(F32)
    grad_keyval_ref[...] = keyval[0].astype(F32)
    grad_down_ref[...] = split[0].astype(F32)
    grad_up_ref[...] = split[1].astype(F32)
    for index, vector in enumerate(vector_refs):
        rows = [small[0, 16 * k + index : 16 * k + index + 1] for k in range(pl.num_programs(0))]
        vector[...] = jnp.concatenate(rows, axis=1).astype(F32).reshape(vector.shape)


def shards(
    dp,
    tokens,
    cotangent,
    tags,
    tag_weight,
    query_weight,
    key_value_weight,
    output_weight,
    up_weight,
    down_weight,
    norm_gain_one,
    norm_bias_one,
    norm_gain_two,
    norm_bias_two,
):
    plan = Plan(dp)
    _, own_len, width = tokens.shape
    full_len = 4 * own_len
    q_cols, kv_cols, hidden = query_weight.shape[1], key_value_weight.shape[1], up_weight.shape[1]
    heads = q_cols // HD
    wide = heads * TILE
    blocks, own_blocks = full_len // TILE, own_len // TILE
    frequencies = (10000.0 ** (-np.arange(0, ROT, 2, dtype=np.float32) / ROT)).astype(np.float32)
    angles = frequencies[:, None] * np.arange(full_len, dtype=np.float32)[None, :]
    table = np.concatenate([np.cos(angles), np.sin(angles)], axis=0).astype(np.float32)

    slices = width // LANES
    units = 2 * slices + 4
    small_rows = LANES
    extra = max(1, len(plan.extra))
    vmem = lambda *shape, kind=BF: pltpu.VMEM(shape, kind)
    dma = lambda *shape: pltpu.SemaphoreType.DMA(shape)
    scratch = [
        vmem(2 * blocks, width, LANES),
        vmem(2 * blocks, width, LANES),
        vmem(2 * blocks, width, LANES),
        vmem(2 * blocks, width, LANES),
        vmem(2 * blocks, width, LANES),
        vmem(hidden, width),
        vmem(width, hidden),
        vmem(q_cols + kv_cols, width),
        vmem(width, q_cols + kv_cols),
        vmem(width, q_cols),
        vmem(2 * blocks, HD, wide // 2),
        vmem(HD, full_len),
        vmem(blocks, TILE, HD),
        vmem(HD + 16, full_len),
        vmem(blocks, TILE, HD),
        vmem(2 * blocks, HD, wide // 2),
        vmem(blocks, q_cols + kv_cols, TILE),
        vmem(width, 8, kind=F32),
        vmem(8, width, kind=F32),
        vmem(width, LANES, kind=F32),
        vmem(q_cols, width, kind=F32),
        vmem(q_cols + kv_cols, width, kind=F32),
        vmem(blocks, TILE, wide, kind=F32),
        vmem(blocks, TILE, wide),
        vmem(HD + 16, wide, kind=F32),
        vmem(HD, full_len, kind=F32),
        vmem(HD, full_len, kind=F32),
        vmem(units, width, LANES),
        vmem(units, width - width // 8, LANES),
        vmem(units, extra, width // 8, LANES),
        vmem(1, small_rows, LANES),
        vmem(1, small_rows - small_rows // 8, LANES),
        vmem(1, extra, small_rows // 8, LANES),
        vmem(4, width // 8, LANES),
        vmem(4, small_rows // 8, LANES),
        vmem(2, blocks // 2, 2, width // 2, LANES),
        vmem(2, own_blocks, 2, width, LANES),
        vmem(2, own_blocks, 2, width, LANES),
        dma(2, own_blocks, 2, 3),
        dma(2, own_blocks, 2, 3),
        dma(2, blocks),
        dma(2, blocks),
        dma(2, blocks),
        dma(2, own_blocks, 2),
        dma(units, plan.stages),
        dma(units, plan.stages),
        dma(1, plan.stages),
        dma(1, plan.stages),
        dma(2, 3),
        dma(2, 3),
    ]
    in_vmem = pl.BlockSpec(memory_space=pltpu.VMEM)
    in_smem = pl.BlockSpec(memory_space=pltpu.SMEM)
    block_out, grad_tokens, total, total_small = pl.pallas_call(
        functools.partial(block_kernel, plan),
        out_shape=(
            jax.ShapeDtypeStruct((width, own_len), BF),
            jax.ShapeDtypeStruct((width, own_len), BF),
            jax.ShapeDtypeStruct((units, width, LANES), BF),
            jax.ShapeDtypeStruct((1, small_rows, LANES), BF),
        ),
        in_specs=[in_smem] * 2 + [in_vmem] * 12,
        out_specs=(in_vmem,) * 4,
        scratch_shapes=scratch,
        compiler_params=pltpu.CompilerParams(
            collective_id=0, has_side_effects=True, vmem_limit_bytes=63 << 20
        ),
    )(
        tags,
        tag_weight,
        tokens[0],
        cotangent[0],
        query_weight.T,
        key_value_weight,
        output_weight,
        up_weight,
        down_weight,
        norm_gain_one,
        norm_bias_one,
        norm_gain_two,
        norm_bias_two,
        jnp.asarray(table),
    )
    first_end = slices * width // q_cols
    finish_shapes = (
        ((own_len, width), BF),
        ((own_len, width), BF),
        ((q_cols, width), F32),
        ((width, kv_cols), F32),
        ((q_cols, width), F32),
        ((width, hidden), F32),
        ((hidden, width), F32),
        ((width,), F32),
        ((width,), F32),
        ((width,), F32),
        ((width,), F32),
    )
    by_columns = lambda rows: pl.BlockSpec((rows, LANES), lambda i: (0, i))
    by_rows = pl.BlockSpec((LANES, own_len), lambda i: (i, 0))
    block_out, grad_tokens, grad_query, grad_keyval, grad_output, grad_up, grad_down, *vectors = (
        pl.pallas_call(
            finish_kernel,
            grid=(slices,),
            out_shape=tuple(jax.ShapeDtypeStruct(*shape) for shape in finish_shapes),
            in_specs=[
                by_rows,
                by_rows,
                pl.BlockSpec((2, width, LANES), lambda i: (i, 0, 0)),
                pl.BlockSpec((2, q_cols, LANES), lambda i: (first_end + i, 0, 0)),
                pl.BlockSpec((1, width, LANES), lambda i: (2 * slices + 3, 0, 0)),
                pl.BlockSpec((1, small_rows, LANES), lambda i: (0, 0, 0)),
            ],
            out_specs=(
                by_columns(own_len),
                by_columns(own_len),
                by_columns(q_cols),
                pl.BlockSpec((width, kv_cols), lambda i: (0, 0)),
                by_columns(q_cols),
                by_columns(width),
                by_columns(hidden),
                pl.BlockSpec((width,), lambda i: (0,)),
                pl.BlockSpec((width,), lambda i: (0,)),
                pl.BlockSpec((width,), lambda i: (0,)),
                pl.BlockSpec((width,), lambda i: (0,)),
            ),
            compiler_params=pltpu.CompilerParams(vmem_limit_bytes=60 << 20),
        )(
            block_out,
            grad_tokens,
            total,
            total.reshape(units * width // q_cols, q_cols, LANES),
            total,
            total_small,
        )
    )
    return (
        block_out[None],
        grad_tokens[None],
        grad_query.T,
        grad_keyval,
        grad_output,
        grad_up,
        grad_down,
        *vectors,
    )


def solution(mesh):
    rows = P("dp", "tp", None)
    columns, depth, whole = P(None, "tp"), P("tp", None), P()
    in_specs = (rows, rows, P("dp"), whole, columns, whole, depth, columns, depth) + (whole,) * 4
    out_specs = (rows, rows, columns, whole, depth, columns, depth) + (whole,) * 4
    return jax.shard_map(
        functools.partial(shards, mesh.shape["dp"]),
        mesh=mesh,
        in_specs=in_specs,
        out_specs=out_specs,
        check_vma=False,
    )
```

time: 195 us -> 165 us (0.85)
  local copies, waits for them, and re-layouts: 27.5 us -> 0 us
  other arithmetic: 2.07 us -> 0 us
    unnamed x9 -> x0, local copies, waits for them, and re-layouts: 13.3 us -> none
    another operation x6 -> x0, local copies, waits for them, and re-layouts: 7.63 us -> none  [the longest x1 4.22 us: shards(): grad_downward, grad_upward = split.reshape(2, width, width).astype(F32)]
    pallas_call x1, Pallas kernels: 163 us -> 156 us  [shards(): pl.pallas_call(functools.partial(block_kernel, plan), out_shape=(jax.Shap...]
    pallas_call x0 -> x1, Pallas kernels: none -> 6.87 us  [shards(): pl.pallas_call(finish_kernel, grid=(slices,), out_shape=tuple((jax.ShapeD...]
    slice x5 -> x0, local copies, waits for them, and re-layouts: 3.59 us -> none  [the longest x1 1.82 us: shards(): total[:2 * slices].reshape(slices, 2, width, LANES).transpose(1, 2, 0, 3)]
    convert_element_type x1 -> x0, local copies, waits for them, and re-layouts: 3 us -> none  [shards(): grad_downward, grad_upward = split.reshape(2, width, width).astype(F32)]
    convert_element_type x3 -> x0, other arithmetic: 2.07 us -> none  [the longest x1 1.7 us: shards(): grad_keyval = total[2 * slices + 3].astype(F32)]
where the time goes in v3:
time: 165 us; the launch traced here: 164 us
  Pallas kernels  163 us (99%)
    pallas_call x1, Pallas kernels, shards(): pl.pallas_call(functools.partial(block_kernel, plan), out_shape=(jax.Shap...  156 us
    pallas_call x1, Pallas kernels, shards(): pl.pallas_call(finish_kernel, grid=(slices,), out_shape=tuple((jax.ShapeD...  6.87 us

profile of v3, /device:TPU:0, one launch (start us, length us, event | category | flops | bytes accessed | tf_op | source)
XLA Modules:
  0.0 164.2 jit_solution(18436426017740691883)
XLA Ops:
  1.3 155.9 %shard_map.221 = (bf16[768,512]{1,0:T(8,128)(2,1)}, bf16[768,512]{1,0:T(8,128)(2,1)}, bf16[16,768,128]{2,1,0:T(8,128)(2,1)}, bf16[1,128,128]{2,1,0:T(8,128)(2,1)}) custom-call(s32[1]{0:T(128)S(6)} %copy.25.tags_ref, f32[8]{0:T(128)} %tag_weight_ref.1, bf16[512,768]{1,0:T(8,128)(2,1)} %bitcast.8, bf16[512,768]{1,0:T(8,128)(2,1)} %bitcast.9, ...), custom_call_target="tpu_custom_call" | custom-call | tf_op jit(solution)/shard_map/pallas_call | solution.py:808
  157.2 6.9 %shard_map.222 = (bf16[512,768]{1,0:T(8,128)(2,1)}, bf16[512,768]{1,0:T(8,128)(2,1)}, f32[192,768]{1,0:T(8,128)}, f32[768,128]{1,0:T(8,128)}, f32[192,768]{1,0:T...) custom-call(bf16[768,512]{1,0:T(8,128)(2,1)} %get-tuple-element.26.b, ...), custom_call_target="tpu_custom_call" | custom-call | tf_op jit(solution)/shard_map/pallas_call | solution.py:855

commit v4 on v3

--- a/solution.py
+++ b/solution.py
@@ -13,6 +13,7 @@
 HALF = ROT // 2
 TILE = 256
 LANES = 128
+RING = 8
 MESH = pl.DeviceIdType.MESH
 BF = jnp.bfloat16
 F32 = jnp.float32
@@ -38,8 +39,8 @@
         self.bits = dp.bit_length() - 1
         self.extra = [2**position for position in range(3, self.bits)]
         self.stages = 6 + len(self.extra)
-        self.lag = [1 + 2 * stage for stage in range(self.stages - 1)]
-        self.lag.append(self.lag[-1] + 4)
+        self.steps = 2 * (RING - 1) + len(self.extra)
+        self.slots = 2 * (self.steps + 1)
 
     def strides(self, kind):
         return (1 + kind, 2 - kind, 4)
@@ -112,6 +113,101 @@
                 self.total[unit, pl.ds(start, size)] = summed
             else:
                 self.part[unit, pl.ds(start, size)] = summed
+
+
+class Ring:
+    def __init__(self, plan, d, t, part, landed, swapped, total, send, recv, height):
+        self.plan, self.d, self.t = plan, d, t
+        self.part, self.landed, self.swapped, self.total = part, landed, swapped, total
+        self.send, self.recv = send, recv
+        self.height = height
+        self.rows = part.shape[1] // RING
+        self.first = d - d % RING
+        line, side = (d % RING) // 2, d % 2
+        self.place = line + side * (RING - 1 - 2 * line)
+
+    def device(self, place):
+        far = place // (RING // 2)
+        return self.first + (1 - far) * 2 * place + far * (2 * RING - 1 - 2 * place)
+
+    def neighbour(self, way):
+        return self.device((self.place + (1, RING - 1)[way]) % RING)
+
+    def units(self, way, sub):
+        return pl.ds((2 * way + sub) * self.height, self.height)
+
+    def chunk(self, way, ahead):
+        index = (self.place + RING + (1, -1)[way] * ahead) % RING
+        return pl.ds(pl.multiple_of(index * self.rows, 16), self.rows)
+
+    def copy(self, way, sub, phase, index, step):
+        units = self.units(way, sub)
+        peer = self.neighbour(way)
+        if phase == 0:
+            source = self.part.at[units, self.chunk(way, -index)]
+            slot = pl.ds(pl.multiple_of(index * self.rows, 16), self.rows)
+            target = self.landed.at[units, slot]
+        elif phase == 1:
+            stride = self.plan.extra[index]
+            peer = self.d + (1 - 2 * ((self.d // stride) % 2)) * stride
+            source = self.part.at[units, self.chunk(way, 1)]
+            target = self.swapped.at[units, index]
+        else:
+            source = self.total.at[units, self.chunk(way, 1 - index)]
+            target = source
+        return pltpu.make_async_remote_copy(
+            src_ref=source,
+            dst_ref=target,
+            send_sem=self.send.at[2 * way + sub, step],
+            recv_sem=self.recv.at[2 * way + sub, step],
+            device_id=(peer, self.t),
+            device_id_type=MESH,
+        )
+
+    def finish(self, way, sub, phase, index, step):
+        self.copy(way, sub, phase, index, step).wait()
+        if phase == 2:
+            return
+        units = self.units(way, sub)
+        if phase == 0:
+            slot = pl.ds(pl.multiple_of(index * self.rows, 16), self.rows)
+            rows, arrived = self.chunk(way, -1 - index), self.landed[units, slot]
+        else:
+            rows, arrived = self.chunk(way, 1), self.swapped[units, index]
+        summed = (self.part[units, rows].astype(F32) + arrived.astype(F32)).astype(BF)
+        self.part[units, rows] = summed
+        if phase == 1:
+            if index == len(self.plan.extra) - 1:
+                self.total[units, rows] = summed
+        elif not self.plan.extra:
+
+            @pl.when(index == RING - 2)
+            def _():
+                self.total[units, rows] = summed
+
+    def slot(self, number):
+        sub = number % 2
+        extra = len(self.plan.extra)
+        middle = RING - 1 + extra
+
+        def act(step, method):
+            @pl.when((step >= 0) & (step < RING - 1))
+            def _():
+                method(way, sub, 0, step, step)
+
+            for index in range(extra):
+
+                @pl.when(step == RING - 1 + index)
+                def _():
+                    method(way, sub, 1, index, step)
+
+            @pl.when((step >= middle) & (step < self.plan.steps))
+            def _():
+                method(way, sub, 2, step - middle, step)
+
+        for way in range(2):
+            act(number // 2 - 1, self.finish)
+            act(number // 2, lambda *where: self.copy(*where).start())
 
 
 def block_kernel(
@@ -150,7 +246,8 @@
     v_t,
     v_r,
     do_t,
-    gq_all,
+    gkv_all,
+    kv_land,
     norms_c,
     norms_r,
     bias_acc,
@@ -178,12 +275,16 @@
     rs_recv,
     rs_send_x,
     rs_recv_x,
+    ring_send,
+    ring_recv,
     dp_send,
     dp_recv,
     dp_send_small,
     dp_recv_small,
     tp_send,
     tp_recv,
+    kv_send,
+    kv_recv,
 ):
     d, t = lax.axis_index("dp"), lax.axis_index("tp")
     chip, core = t // 2, t % 2
@@ -199,13 +300,19 @@
     half_width = width // 2
     tall = width // TILE
 
+    slices = width // LANES
+    base = 2 * slices
     big = Bundle(plan, d, t, part, landed, swapped, total_ref, dp_send, dp_recv)
+    ring = Ring(
+        plan, d, t, part, landed, swapped, total_ref, ring_send, ring_recv, slices // 2
+    )
     small = Bundle(
         plan, d, t, part_small, landed_small, swapped_small, total_small_ref, dp_send_small, dp_recv_small
     )
 
     barrier = pltpu.get_barrier_semaphore()
     peers = [(d, sib), (d, across), (d, diag)] + [(big.partner(2**b), t) for b in range(plan.bits)]
+    peers += [(ring.neighbour(way), t) for way in range(2)]
     for peer in peers:
         pl.semaphore_signal(barrier, inc=1, device_id=peer, device_id_type=MESH)
     pl.semaphore_wait(barrier, len(peers))
@@ -330,17 +437,31 @@
             k_r[place, half_lanes(0, half), :] = key[:, side].T.astype(BF)
             v_r[place, half_lanes(0, half), :] = value[:, side].T.astype(BF)
 
-        pre_act = mm(up_t[...], n2)
-        cdf = 0.5 + 0.5 * lax.erf(pre_act * 0.7071067811865476)
-        density = jnp.exp(-0.5 * pre_act * pre_act) * 0.3989422804014327
-        middle = (pre_act * cdf).astype(BF)
-        slope = cdf + pre_act * density
+        chunks = [slice(c * TILE, (c + 1) * TILE) for c in range(tall)]
+
+        def activate(pre_act):
+            cdf = 0.5 + 0.5 * lax.erf(pre_act * 0.7071067811865476)
+            density = jnp.exp(-0.5 * pre_act * pre_act) * 0.3989422804014327
+            return (pre_act * cdf).astype(BF), cdf + pre_act * density
+
+        pre_acts = [mm(up_t[chunks[0], :], n2)]
+        grad_mids, middles, grads = [], [], []
+        for c in range(tall):
+            grad_mids.append(mm(down_ref[chunks[c], :], gr))
+            if c + 1 < tall:
+                pre_acts.append(mm(up_t[chunks[c + 1], :], n2))
+            middle, slope = activate(pre_acts[c])
+            middles.append(middle)
+            grads.append((grad_mids[c] * slope).astype(BF))
+            if c > 0:
+                score[c - 1] += mm_t(middles[c - 1], gr)
+        middle = jnp.concatenate(middles, axis=0)
+        grad_hidden = jnp.concatenate(grads, axis=0)
+        score[tall - 1] += mm_t(middles[-1], gr)
         store(br_all, mm(down_t[...], middle).astype(BF))
-        grad_hidden = (mm(down_ref[...], gr) * slope).astype(BF)
         up_two = mm(up_ref[...], grad_hidden)
         bias_acc[...] += up_two[:, :LANES] + up_two[:, LANES:]
         store(g_all, (up_two * norms_c[:, 2:3]).astype(BF))
-        score[:tall] += mm_t(middle, gr).reshape(tall, TILE, width)
         score[tall : 2 * tall] += mm_t(n2, grad_hidden).reshape(tall, TILE, hidden)
         return carry
 
@@ -356,13 +477,12 @@
 
     lax.fori_loop(0, 2 * own_blocks, gathered, 0)
 
-    slices = width // LANES
-    for index in range(slices):
-        cols = slice(index * LANES, (index + 1) * LANES)
-        part[2 * index] = score[:tall, :, cols].reshape(hidden, LANES).astype(BF)
-        big.start(2 * index, (2 * index) % 4 // 3, 0)
-        part[2 * index + 1] = score[tall : 2 * tall, :, cols].reshape(width, LANES).astype(BF)
-        big.start(2 * index + 1, (2 * index + 1) % 4 // 3, 0)
+    for first in range(2):
+        for index in range(first * slices // 2, (first + 1) * slices // 2):
+            cols = slice(index * LANES, (index + 1) * LANES)
+            part[index] = score[:tall, :, cols].reshape(hidden, LANES).astype(BF)
+            part[slices + index] = score[tall : 2 * tall, :, cols].reshape(width, LANES).astype(BF)
+        ring.slot(first)
     for index in range(tall):
         rows = slice(index * TILE, (index + 1) * TILE)
         product = jnp.sum(up_ref[rows, :].astype(F32) * score[tall + index], axis=1, keepdims=True)
@@ -373,7 +493,7 @@
     outs = (br_all, g_all)
 
     def block_of(step):
-        return (blocks - 1) - step // 2 - (blocks // 2) * (step % 2)
+        return step // 2 + (blocks // 2) * (step % 2)
 
     def pre_copy(kind, step, block):
         rows = pl.ds(pl.multiple_of((1 - core) * half_width, 16), half_width)
@@ -445,7 +565,7 @@
 
     def scatter_arrived(kind, piece):
         block = t * own_blocks + piece
-        step = 2 * ((blocks - 1 - block) % (blocks // 2)) + 1 - block // (blocks // 2)
+        step = 2 * (block % (blocks // 2)) + block // (blocks // 2)
         sib_copy(kind, step, block).wait_recv()
         for sender_core in range(2):
             x_copy(kind, block, sender_core, t).wait_recv()
@@ -464,7 +584,14 @@
 
     def emit_grad_tokens(piece):
         place = t * own_blocks + piece
-        scaled = scatter_arrived(1, piece)
+        if piece == 0:
+            for hop in range(3):
+                kv_copy(t, hop, (t + hop + 1) % 4).wait_recv()
+        key_value_grad = gkv_all[place].astype(F32)
+        for hop in range(3):
+            key_value_grad = key_value_grad + kv_land[hop, piece].astype(F32)
+        up_kv = mm(qkv_w[:, q_cols:], key_value_grad.astype(BF))
+        scaled = scatter_arrived(1, piece) + up_kv * norms_c[:, 0:1]
         normal, inverse = standardize(pair(x_all, place).astype(F32))
         mean_one = jnp.sum(scaled, axis=0, keepdims=True) * (1.0 / width)
         mean_two = jnp.sum(scaled * normal, axis=0, keepdims=True) * (1.0 / width)
@@ -472,24 +599,28 @@
             pair(gr_all, place).astype(F32) + inverse * (scaled - mean_one - normal * mean_two)
         ).astype(BF)
 
-    base = 2 * slices
-
-    def slot(index):
-        for stage in reversed(range(plan.stages)):
-            unit = index - plan.lag[stage]
-
-            @pl.when((unit >= 0) & (unit < base))
-            def _():
-                kind = (unit % 4) // 3
-                big.finish(unit, kind, stage)
-                if stage + 1 < plan.stages:
-                    big.start(unit, kind, stage + 1)
-
     def attend(step, carry):
-        slot(3 * step)
+        heavy = step % 2
+        turn_slot = 6 * (step // 2) + 2
+
+        def ring_point(light_slot, heavy_slot):
+            if light_slot is None:
+
+                @pl.when(heavy == 1)
+                def _():
+                    ring.slot(turn_slot + heavy_slot)
+            else:
+                ring.slot(turn_slot + light_slot + heavy * (heavy_slot - light_slot))
+
+        ring_point(None, 2)
         block = block_of(step)
         queries = jnp.concatenate([q_t[2 * block], q_t[2 * block + 1]], axis=1)
         wide = heads * TILE
+
+        def of_head(value, head):
+            first = value[:, head * LANES : (head + 1) * LANES]
+            second = value[:, (heads + head) * LANES : (heads + head + 1) * LANES]
+            return jnp.concatenate([first, second], axis=1)
 
         def in_pairs(count, body, start):
             carry = lax.fori_loop(0, count // 4, lambda i, c: body(4 * i, 4, c), start)
@@ -515,7 +646,7 @@
         top = jnp.max(top, axis=0, keepdims=True)
 
         acc[...] = jnp.zeros_like(acc)
-        slot(3 * step + 1)
+        ring_point(0, 3)
 
         def weigh(j, tiles, carry):
             weights = jnp.exp(score[pl.ds(j, tiles)] - top).astype(BF)
@@ -530,7 +661,16 @@
         delta = jnp.sum(grad.astype(F32) * context, axis=0, keepdims=True)
         acc[:HD] = jnp.zeros((HD, wide), F32)
 
-        slot(3 * step + 2)
+        context_rows = jnp.concatenate([of_head(context, h) for h in range(heads)], axis=0).astype(BF)
+        branch = mm(out_t[...], context_rows) + pair(br_all, block).astype(F32)
+        put_pair(br_all, block, branch.astype(BF))
+        scatter_first(0, step)
+
+        @pl.when(step > 0)
+        def _():
+            scatter_second(1, step - 1)
+
+        ring_point(None, 4)
 
         def back(j, tiles, carry):
             weights = prob[pl.ds(j, tiles)].reshape(tiles * TILE, wide)
@@ -544,95 +684,75 @@
         in_pairs(block + 1, back, 0)
         lanes = pl.ds(pl.multiple_of(block * TILE, TILE), TILE)
         cosine, sine = table_ref[:HALF, lanes], table_ref[HALF:, lanes]
-        def of_head(value, head):
-            first = value[:, head * LANES : (head + 1) * LANES]
-            second = value[:, (heads + head) * LANES : (heads + head + 1) * LANES]
-            return jnp.concatenate([first, second], axis=1)
-
         grad_queries = acc[:HD]
-        for head in range(heads):
-            turned = turn(of_head(grad_queries, head), cosine, -sine) * (HD**-0.5)
-            gq_all[block, head * HD : (head + 1) * HD] = turned.astype(BF)
-        context = jnp.concatenate([of_head(context, h) for h in range(heads)], axis=0).astype(BF)
-        branch = mm(out_t[...], context) + pair(br_all, block).astype(F32)
-        put_pair(br_all, block, branch.astype(BF))
-        sum_out[...] += mm_t(context, pair(gr_all, block))
-        sum_qkv[:q_cols] += mm_t(gq_all[block, :q_cols], pair(n1_all, block))
-        scatter_first(0, step)
-
-        @pl.when(step > 0)
-        def _():
-            scatter_second(0, step - 1)
-
+        turned = [
+            turn(of_head(grad_queries, head), cosine, -sine) * (HD**-0.5) for head in range(heads)
+        ]
+        turned = jnp.concatenate(turned, axis=0).astype(BF)
+        scatter_second(0, step)
+        ring_point(1, 5)
+        scaled = mm(qkv_w[:, :q_cols], turned) * norms_c[:, 0:1] + pair(g_all, block).astype(F32)
+        put_pair(g_all, block, scaled.astype(BF))
+        scatter_first(1, step)
+        sum_out[...] += mm_t(context_rows, pair(gr_all, block))
+        sum_qkv[:q_cols] += mm_t(turned, pair(n1_all, block))
+        bias_acc[:q_cols] += turned[:, :LANES].astype(F32) + turned[:, LANES:].astype(F32)
         return carry
 
     lax.fori_loop(0, blocks, attend, 0)
-    scatter_second(0, blocks - 1)
+    scatter_second(1, blocks - 1)
+
+    def key_value(block, carry):
+        lanes = pl.ds(pl.multiple_of(block * TILE, TILE), TILE)
+        cosine, sine = table_ref[:HALF, lanes], table_ref[HALF:, lanes]
+        gkv_all[block, :HD] = turn(d_key[:, lanes], cosine, -sine).astype(BF)
+        gkv_all[block, HD:] = d_value[:, lanes].astype(BF)
+        grads = gkv_all[block]
+        bias_acc[q_cols : q_cols + 2 * HD] += grads[:, :LANES].astype(F32) + grads[:, LANES:].astype(F32)
+        sum_qkv[q_cols:] += mm_t(grads, pair(n1_all, block))
+        return carry
+
+    lax.fori_loop(0, blocks, key_value, 0)
+
+    def kv_copy(owner, hop, target):
+        return pltpu.make_async_remote_copy(
+            src_ref=gkv_all.at[pl.ds(owner * own_blocks, own_blocks)],
+            dst_ref=kv_land.at[hop],
+            send_sem=kv_send.at[hop],
+            recv_sem=kv_recv.at[hop],
+            device_id=(d, target),
+            device_id_type=MESH,
+        )
+
+    for hop in range(3):
+        owner = (t + hop + 1) % 4
+        kv_copy(owner, hop, owner).start()
 
     for index in range(slices):
         cols = slice(index * LANES, (index + 1) * LANES)
         for which, source in ((0, sum_out[:, cols]), (1, sum_qkv[:q_cols, cols])):
             row = (2 * index + which) * q_cols
             part[base + row // width, row % width : row % width + q_cols] = source.astype(BF)
-    first_ends = [(big, base, 0), (big, base + 1, 1), (big, base + 2, 0)]
-    for bundle, unit, kind in first_ends:
+    part[base + 3] = sum_qkv[q_cols:].T.astype(BF)
+    ends = [(big, base + unit, unit % 2) for unit in range(4)] + [(small, 0, 0)]
+    for bundle, unit, kind in ends[:4]:
         bundle.start(unit, kind, 0)
-
-    def project(step, carry):
-        slot(3 * blocks + step)
-        block = block_of(step)
-        lanes = pl.ds(pl.multiple_of(block * TILE, TILE), TILE)
-        cosine, sine = table_ref[:HALF, lanes], table_ref[HALF:, lanes]
-        gq_all[block, q_cols : q_cols + HD] = turn(d_key[:, lanes], cosine, -sine).astype(BF)
-        gq_all[block, q_cols + HD :] = d_value[:, lanes].astype(BF)
-        grads = gq_all[block]
-        up_one = mm(qkv_w[...], grads)
-        bias_acc[...] += up_one[:, :LANES] + up_one[:, LANES:]
-        put_pair(g_all, block, (pair(g_all, block).astype(F32) + up_one * norms_c[:, 0:1]).astype(BF))
-        sum_qkv[q_cols:] += mm_t(grads[q_cols:], pair(n1_all, block))
-        scatter_first(1, step)
-
-        @pl.when(step > 0)
-        def _():
-            scatter_second(1, step - 1)
-
-        for stage, when in ((0, 4), (1, 7)):
-
-            @pl.when(step == when)
-            def _():
-                for bundle, unit, kind in first_ends:
-                    bundle.finish(unit, kind, stage)
-                    bundle.start(unit, kind, stage + 1)
-
-        return carry
-
-    lax.fori_loop(0, blocks, project, 0)
-    scatter_second(1, blocks - 1)
-    for index in range(4 * blocks, base + plan.lag[-1]):
-        slot(index)
-
-    grad_keyval = sum_qkv[q_cols:].T
-    part[base + 3] = grad_keyval.astype(BF)
-    shift_one = jnp.sum(bias_acc[...], axis=1, keepdims=True)
+    row_sums = jnp.sum(bias_acc[: q_cols + 2 * HD], axis=1, keepdims=True)
+    shift_one = jnp.sum(qkv_t[...].astype(F32) * row_sums, axis=0, keepdims=True)
     shift_two = norms_c[:, 5:6]
     product_one = jnp.sum(qkv_t[...].astype(F32) * sum_qkv[...], axis=0, keepdims=True)
-    product_one = jnp.broadcast_to(product_one, (8, width)).T[:, :1]
-    gain_one = (product_one - norms_c[:, 1:2] * shift_one) / norms_c[:, 0:1]
+    gain_one = (product_one - norms_r[1:2] * shift_one) / norms_r[0:1]
     gain_two = (norms_c[:, 4:5] - norms_c[:, 3:4] * shift_two) / norms_c[:, 2:3]
     lane = lax.broadcasted_iota(jnp.int32, (width, 8), 1)
-    columns = jnp.where(
-        lane == 0, gain_one, jnp.where(lane == 1, shift_one, jnp.where(lane == 2, gain_two, shift_two))
-    )
-    rows = columns.T
+    columns = jnp.where(lane == 0, gain_two, shift_two).T
+    rows = jnp.concatenate([gain_one, shift_one, columns[:6]], axis=0)
     part_small[0] = jnp.zeros(part_small.shape[1:], BF)
     for index in range(slices):
         part_small[0, 16 * index : 16 * index + 8] = rows[
             :, index * LANES : (index + 1) * LANES
         ].astype(BF)
 
-    last_ends = [(big, base + 3, 1), (small, 0, 0)]
-    for bundle, unit, kind in last_ends:
-        bundle.start(unit, kind, 0)
+    small.start(0, 0, 0)
     lands = (tp_land, tp_land_small)
 
     def tp_copy(index, sender, hop):
@@ -646,41 +766,42 @@
         )
 
     middle_stage = 2 + len(plan.extra)
+    ring_slots = list(range(3 * blocks + 2, plan.slots))
     for beat in range(plan.stages + 1):
-        stage = beat + 2
-        if stage < plan.stages:
-            for bundle, unit, kind in first_ends:
-                bundle.finish(unit, kind, stage)
-                if stage + 1 < plan.stages:
-                    bundle.start(unit, kind, stage + 1)
-        for index, (bundle, unit, kind) in enumerate(last_ends):
+        for index in ring_slots[2 * beat : 2 * beat + 2]:
+            ring.slot(index)
+        for index, (bundle, unit, kind) in enumerate(ends):
             rows = pl.ds(*bundle.span(kind, 3))
-            if beat < middle_stage:
-                bundle.finish(unit, kind, beat)
-                bundle.start(unit, kind, beat + 1)
+            shared = index - 3
+            if shared < 0 or beat < middle_stage:
+                if beat < plan.stages:
+                    bundle.finish(unit, kind, beat)
+                if beat + 1 < plan.stages:
+                    bundle.start(unit, kind, beat + 1)
             elif beat == middle_stage:
                 bundle.finish(unit, kind, beat, publish=False)
-                lands[index][t] = bundle.part[unit, rows]
+                lands[shared][t] = bundle.part[unit, rows]
                 for hop in range(3):
-                    tp_copy(index, t, hop).start()
+                    tp_copy(shared, t, hop).start()
             elif beat == middle_stage + 1:
                 for hop in range(3):
-                    tp_copy(index, (t + 3 - hop) % 4, hop).wait_recv()
-                land = [lands[index][sender].astype(F32) for sender in range(4)]
+                    tp_copy(shared, (t + 3 - hop) % 4, hop).wait_recv()
+                land = [lands[shared][sender].astype(F32) for sender in range(4)]
                 bundle.total[unit, rows] = (land[0] + land[1] + land[2] + land[3]).astype(BF)
                 bundle.start(unit, kind, beat)
             else:
                 bundle.finish(unit, kind, beat - 1)
                 if beat < plan.stages:
                     bundle.start(unit, kind, beat)
-        if beat == 0:
-            for piece in range(own_blocks):
-                emit_block_out(piece)
+        if 0 < beat <= own_blocks:
+            emit_block_out(beat - 1)
+        elif 4 <= beat < 4 + own_blocks:
+            emit_grad_tokens(beat - 4)
     for index in range(2):
         for hop in range(3):
             tp_copy(index, t, hop).wait_send()
-    for piece in range(own_blocks):
-        emit_grad_tokens(piece)
+    for hop in range(3):
+        kv_copy((t + hop + 1) % 4, hop, (t + hop + 1) % 4).wait_send()
 
     def drain(step, carry):
         for kind in range(2):
@@ -693,7 +814,8 @@
 def finish_kernel(
     block_out_t,
     grad_tokens_t,
-    split,
+    down,
+    up,
     ends,
     keyval,
     small,
@@ -711,8 +833,8 @@
     grad_output_ref[...] = ends[0].astype(F32)
     grad_query_ref[...] = ends[1].astype(F32)
     grad_keyval_ref[...] = keyval[0].astype(F32)
-    grad_down_ref[...] = split[0].astype(F32)
-    grad_up_ref[...] = split[1].astype(F32)
+    grad_down_ref[...] = down[0].astype(F32)
+    grad_up_ref[...] = up[0].astype(F32)
     for index, vector in enumerate(vector_refs):
         rows = [small[0, 16 * k + index : 16 * k + index + 1] for k in range(pl.num_programs(0))]
         vector[...] = jnp.concatenate(rows, axis=1).astype(F32).reshape(vector.shape)
@@ -768,7 +890,8 @@
         vmem(HD + 16, full_len),
         vmem(blocks, TILE, HD),
         vmem(2 * blocks, HD, wide // 2),
-        vmem(blocks, q_cols + kv_cols, TILE),
+        vmem(blocks, kv_cols, TILE),
+        vmem(4, own_blocks, kv_cols, TILE),
         vmem(width, 8, kind=F32),
         vmem(8, width, kind=F32),
         vmem(width, LANES, kind=F32),
@@ -796,12 +919,16 @@
         dma(2, blocks),
         dma(2, blocks),
         dma(2, own_blocks, 2),
+        dma(4, plan.steps),
+        dma(4, plan.steps),
         dma(units, plan.stages),
         dma(units, plan.stages),
         dma(1, plan.stages),
         dma(1, plan.stages),
         dma(2, 3),
         dma(2, 3),
+        dma(3),
+        dma(3),
     ]
     in_vmem = pl.BlockSpec(memory_space=pltpu.VMEM)
     in_smem = pl.BlockSpec(memory_space=pltpu.SMEM)
@@ -859,7 +986,8 @@
             in_specs=[
                 by_rows,
                 by_rows,
-                pl.BlockSpec((2, width, LANES), lambda i: (i, 0, 0)),
+                pl.BlockSpec((1, width, LANES), lambda i: (i, 0, 0)),
+                pl.BlockSpec((1, width, LANES), lambda i: (slices + i, 0, 0)),
                 pl.BlockSpec((2, q_cols, LANES), lambda i: (first_end + i, 0, 0)),
                 pl.BlockSpec((1, width, LANES), lambda i: (2 * slices + 3, 0, 0)),
                 pl.BlockSpec((1, small_rows, LANES), lambda i: (0, 0, 0)),
@@ -882,6 +1010,7 @@
             block_out,
             grad_tokens,
             total,
+            total,
             total.reshape(units * width // q_cols, q_cols, LANES),
             total,
             total_small,

time: 165 us -> 150 us (0.909)
  Pallas kernels: 163 us -> 149 us
    pallas_call x1, Pallas kernels: 156 us -> 141 us  [shards(): pl.pallas_call(functools.partial(block_kernel, plan), out_shape=(jax.Shap...]
where the time goes in v4:
time: 150 us
  Pallas kernels  149 us (99%)
    pallas_call x1, Pallas kernels, shards(): pl.pallas_call(functools.partial(block_kernel, plan), out_shape=(jax.Shap...  141 us
    pallas_call x1, Pallas kernels, shards(): pl.pallas_call(finish_kernel, grid=(slices,), out_shape=tuple((jax.ShapeD...  7.35 us

profile of v4, /device:TPU:0, one launch (start us, length us, event | category | flops | bytes accessed | tf_op | source)
XLA Modules:
  0.0 150.1 jit_solution(7264782789139347318)
XLA Ops:
  1.3 141.3 %shard_map.221 = (bf16[768,512]{1,0:T(8,128)(2,1)}, bf16[768,512]{1,0:T(8,128)(2,1)}, bf16[16,768,128]{2,1,0:T(8,128)(2,1)}, bf16[1,128,128]{2,1,0:T(8,128)(2,1)}) custom-call(s32[1]{0:T(128)S(6)} %copy.25.tags_ref, f32[8]{0:T(128)} %tag_weight_ref.1, bf16[512,768]{1,0:T(8,128)(2,1)} %bitcast.8, bf16[512,768]{1,0:T(8,128)(2,1)} %bitcast.9, ...), custom_call_target="tpu_custom_call" | custom-call | tf_op jit(solution)/shard_map/pallas_call | solution.py:935
  142.6 7.4 %shard_map.222 = (bf16[512,768]{1,0:T(8,128)(2,1)}, bf16[512,768]{1,0:T(8,128)(2,1)}, f32[192,768]{1,0:T(8,128)}, f32[768,128]{1,0:T(8,128)}, f32[192,768]{1,0:T...) custom-call(bf16[768,512]{1,0:T(8,128)(2,1)} %get-tuple-element.26.b, ...), custom_call_target="tpu_custom_call" | custom-call | tf_op jit(solution)/shard_map/pallas_call | solution.py:982

commit v5 on v4

--- a/solution.py
+++ b/solution.py
@@ -14,6 +14,7 @@
 TILE = 256
 LANES = 128
 RING = 8
+SUBS = 3
 MESH = pl.DeviceIdType.MESH
 BF = jnp.bfloat16
 F32 = jnp.float32
@@ -40,7 +41,7 @@
         self.extra = [2**position for position in range(3, self.bits)]
         self.stages = 6 + len(self.extra)
         self.steps = 2 * (RING - 1) + len(self.extra)
-        self.slots = 2 * (self.steps + 1)
+        self.slots = SUBS * (self.steps + 1)
 
     def strides(self, kind):
         return (1 + kind, 2 - kind, 4)
@@ -125,24 +126,24 @@
         self.first = d - d % RING
         line, side = (d % RING) // 2, d % 2
         self.place = line + side * (RING - 1 - 2 * line)
+        self.neighbours = [
+            self.device(lax.rem(self.place + ahead, jnp.int32(RING))) for ahead in (1, RING - 1)
+        ]
 
     def device(self, place):
         far = place // (RING // 2)
         return self.first + (1 - far) * 2 * place + far * (2 * RING - 1 - 2 * place)
 
-    def neighbour(self, way):
-        return self.device((self.place + (1, RING - 1)[way]) % RING)
-
     def units(self, way, sub):
-        return pl.ds((2 * way + sub) * self.height, self.height)
+        return pl.ds((SUBS * way + sub) * self.height, self.height)
 
     def chunk(self, way, ahead):
-        index = (self.place + RING + (1, -1)[way] * ahead) % RING
+        index = lax.rem(self.place + RING + (1, -1)[way] * ahead, jnp.int32(RING))
         return pl.ds(pl.multiple_of(index * self.rows, 16), self.rows)
 
     def copy(self, way, sub, phase, index, step):
         units = self.units(way, sub)
-        peer = self.neighbour(way)
+        peer = self.neighbours[way]
         if phase == 0:
             source = self.part.at[units, self.chunk(way, -index)]
             slot = pl.ds(pl.multiple_of(index * self.rows, 16), self.rows)
@@ -158,14 +159,13 @@
         return pltpu.make_async_remote_copy(
             src_ref=source,
             dst_ref=target,
-            send_sem=self.send.at[2 * way + sub, step],
-            recv_sem=self.recv.at[2 * way + sub, step],
+            send_sem=self.send.at[SUBS * way + sub, step],
+            recv_sem=self.recv.at[SUBS * way + sub, step],
             device_id=(peer, self.t),
             device_id_type=MESH,
         )
 
-    def finish(self, way, sub, phase, index, step):
-        self.copy(way, sub, phase, index, step).wait()
+    def finish(self, way, sub, phase, index, step, last):
         if phase == 2:
             return
         units = self.units(way, sub)
@@ -175,45 +175,59 @@
         else:
             rows, arrived = self.chunk(way, 1), self.swapped[units, index]
         summed = (self.part[units, rows].astype(F32) + arrived.astype(F32)).astype(BF)
-        self.part[units, rows] = summed
-        if phase == 1:
-            if index == len(self.plan.extra) - 1:
-                self.total[units, rows] = summed
-        elif not self.plan.extra:
-
-            @pl.when(index == RING - 2)
+        (self.total if last else self.part)[units, rows] = summed
+
+    def slot(self, number):
+        number = jnp.int32(number)
+        step = lax.div(number, jnp.int32(SUBS))
+        sub = number - step * SUBS
+        extra = len(self.plan.extra)
+        turns = RING - 1
+        middle = turns + extra
+
+        def when(condition, ended, begun, last=False):
+            @pl.when(condition)
             def _():
-                self.total[units, rows] = summed
-
-    def slot(self, number):
-        sub = number % 2
-        extra = len(self.plan.extra)
-        middle = RING - 1 + extra
-
-        def act(step, method):
-            @pl.when((step >= 0) & (step < RING - 1))
-            def _():
-                method(way, sub, 0, step, step)
-
-            for index in range(extra):
-
-                @pl.when(step == RING - 1 + index)
-                def _():
-                    method(way, sub, 1, index, step)
-
-            @pl.when((step >= middle) & (step < self.plan.steps))
-            def _():
-                method(way, sub, 2, step - middle, step)
-
-        for way in range(2):
-            act(number // 2 - 1, self.finish)
-            act(number // 2, lambda *where: self.copy(*where).start())
+                if ended is not None:
+                    for way in range(2):
+                        self.copy(way, sub, *ended, step - 1).wait()
+                        self.finish(way, sub, *ended, step - 1, last)
+                        if begun is not None:
+                            self.copy(way, sub, *begun, step).start()
+                else:
+                    for way in range(2):
+                        self.copy(way, sub, *begun, step).start()
+
+        when(step == 0, None, (0, 0))
+        when((step > 0) & (step < turns), (0, step - 1), (0, step))
+        for index in range(extra + 1):
+            ended = (0, turns - 1) if index == 0 else (1, index - 1)
+            begun = (2, 0) if index == extra else (1, index)
+            when(step == turns + index, ended, begun, last=index == extra)
+        when((step > middle) & (step < self.plan.steps), (2, step - 1 - middle), (2, step - middle))
+        when(step == self.plan.steps, (2, turns - 1), None)
 
 
 def block_kernel(
     plan,
     tags_ref,
     tag_weight_ref,
+    tok_hbm,
+    cot_hbm,
+    query_t_hbm,
+    keyval_hbm,
+    output_hbm,
+    up_hbm,
+    down_hbm,
+    gain_one_ref,
+    bias_one_ref,
+    gain_two_ref,
+    bias_two_ref,
+    table_hbm,
+    block_out_hbm,
+    grad_tokens_hbm,
+    total_hbm,
+    end_total_hbm,
     tok_ref,
     cot_ref,
     query_t_ref,
@@ -221,15 +235,13 @@
     output_ref,
     up_ref,
     down_ref,
-    gain_one_ref,
-    bias_one_ref,
-    gain_two_ref,
-    bias_two_ref,
     table_ref,
     block_out_ref,
     grad_tokens_ref,
     total_ref,
-    total_small_ref,
+    end_total_ref,
+    load_sem,
+    store_sem,
     x_all,
     gr_all,
     n1_all,
@@ -261,11 +273,10 @@
     part,
     landed,
     swapped,
-    part_small,
-    landed_small,
-    swapped_small,
+    end_part,
+    end_land,
+    end_swap,
     tp_land,
-    tp_land_small,
     pre,
     from_sib,
     from_x,
@@ -279,8 +290,8 @@
     ring_recv,
     dp_send,
     dp_recv,
-    dp_send_small,
-    dp_recv_small,
+    end_send,
+    end_recv,
     tp_send,
     tp_recv,
     kv_send,
@@ -304,15 +315,32 @@
     base = 2 * slices
     big = Bundle(plan, d, t, part, landed, swapped, total_ref, dp_send, dp_recv)
     ring = Ring(
-        plan, d, t, part, landed, swapped, total_ref, ring_send, ring_recv, slices // 2
+        plan, d, t, part, landed, swapped, total_ref, ring_send, ring_recv, slices // SUBS
     )
-    small = Bundle(
-        plan, d, t, part_small, landed_small, swapped_small, total_small_ref, dp_send_small, dp_recv_small
-    )
+
+    loads = [
+        pltpu.make_async_copy(source, target, load_sem.at[index])
+        for index, (source, target) in enumerate(
+            (
+                (tok_hbm, tok_ref),
+                (cot_hbm, cot_ref),
+                (up_hbm, up_ref),
+                (down_hbm, down_ref),
+                (query_t_hbm, query_t_ref),
+                (keyval_hbm, keyval_ref),
+                (output_hbm, output_ref),
+                (table_hbm, table_ref),
+            )
+        )
+    ]
+    for load in loads:
+        load.start()
 
     barrier = pltpu.get_barrier_semaphore()
-    peers = [(d, sib), (d, across), (d, diag)] + [(big.partner(2**b), t) for b in range(plan.bits)]
-    peers += [(ring.neighbour(way), t) for way in range(2)]
+    first_of_ring, spot = d - d % RING, d % RING
+    ring_peers = [first_of_ring + (spot + hop) % RING for hop in range(1, RING)]
+    extra_peers = [d + (1 - 2 * ((d // stride) % 2)) * stride for stride in plan.extra]
+    peers = [(d, sib), (d, across), (d, diag)] + [(peer, t) for peer in ring_peers + extra_peers]
     for peer in peers:
         pl.semaphore_signal(barrier, inc=1, device_id=peer, device_id_type=MESH)
     pl.semaphore_wait(barrier, len(peers))
@@ -344,6 +372,8 @@
             device_id_type=MESH,
         )
 
+    loads[0].wait()
+    loads[1].wait()
     for piece in range(own_blocks):
         rows = slice(piece * TILE, (piece + 1) * TILE)
         put_pair(x_all, t * own_blocks + piece, tok_ref[rows, :].T)
@@ -358,6 +388,8 @@
         gather_copy(0, piece, 1, t, 1).start()
         gather_copy(1, piece, 1, t, 1).start()
 
+    for load in loads[2:]:
+        load.wait()
     up_t[...] = up_ref[...].T
     down_t[...] = down_ref[...].T
     qkv_t[:q_cols] = query_t_ref[...]
@@ -477,8 +509,8 @@
 
     lax.fori_loop(0, 2 * own_blocks, gathered, 0)
 
-    for first in range(2):
-        for index in range(first * slices // 2, (first + 1) * slices // 2):
+    for first in range(SUBS):
+        for index in range(first * slices // SUBS, (first + 1) * slices // SUBS):
             cols = slice(index * LANES, (index + 1) * LANES)
             part[index] = score[:tall, :, cols].reshape(hidden, LANES).astype(BF)
             part[slices + index] = score[tall : 2 * tall, :, cols].reshape(width, LANES).astype(BF)
@@ -599,20 +631,10 @@
             pair(gr_all, place).astype(F32) + inverse * (scaled - mean_one - normal * mean_two)
         ).astype(BF)
 
-    def attend(step, carry):
+    def attend(step, number):
         heavy = step % 2
-        turn_slot = 6 * (step // 2) + 2
-
-        def ring_point(light_slot, heavy_slot):
-            if light_slot is None:
-
-                @pl.when(heavy == 1)
-                def _():
-                    ring.slot(turn_slot + heavy_slot)
-            else:
-                ring.slot(turn_slot + light_slot + heavy * (heavy_slot - light_slot))
-
-        ring_point(None, 2)
+        ring.slot(number)
+        number = number + 1
         block = block_of(step)
         queries = jnp.concatenate([q_t[2 * block], q_t[2 * block + 1]], axis=1)
         wide = heads * TILE
@@ -646,7 +668,12 @@
         top = jnp.max(top, axis=0, keepdims=True)
 
         acc[...] = jnp.zeros_like(acc)
-        ring_point(0, 3)
+
+        @pl.when(heavy == 1)
+        def _():
+            ring.slot(number)
+
+        number = number + heavy
 
         def weigh(j, tiles, carry):
             weights = jnp.exp(score[pl.ds(j, tiles)] - top).astype(BF)
@@ -670,18 +697,18 @@
         def _():
             scatter_second(1, step - 1)
 
-        ring_point(None, 4)
-
-        def back(j, tiles, carry):
+
+        def back(j, tiles, number):
+            ring.slot(number)
             weights = prob[pl.ds(j, tiles)].reshape(tiles * TILE, wide)
             grad_probs = mm(v_r[pl.ds(j, tiles)].reshape(tiles * TILE, HD), grad)
             grad_scores = (weights.astype(F32) * (grad_probs - delta)).astype(BF)
             acc[:HD] += mm(k_t[:, lanes_of(j, tiles)], grad_scores)
             d_key[:, lanes_of(j, tiles)] += mm_t(queries, grad_scores)
             d_value[:, lanes_of(j, tiles)] += mm_t(grad, weights)
-            return carry
-
-        in_pairs(block + 1, back, 0)
+            return number + 1
+
+        number = in_pairs(block + 1, back, number)
         lanes = pl.ds(pl.multiple_of(block * TILE, TILE), TILE)
         cosine, sine = table_ref[:HALF, lanes], table_ref[HALF:, lanes]
         grad_queries = acc[:HD]
@@ -690,19 +717,34 @@
         ]
         turned = jnp.concatenate(turned, axis=0).astype(BF)
         scatter_second(0, step)
-        ring_point(1, 5)
+        ring.slot(number)
+        number = number + 1
         scaled = mm(qkv_w[:, :q_cols], turned) * norms_c[:, 0:1] + pair(g_all, block).astype(F32)
         put_pair(g_all, block, scaled.astype(BF))
         scatter_first(1, step)
         sum_out[...] += mm_t(context_rows, pair(gr_all, block))
         sum_qkv[:q_cols] += mm_t(turned, pair(n1_all, block))
         bias_acc[:q_cols] += turned[:, :LANES].astype(F32) + turned[:, LANES:].astype(F32)
-        return carry
-
-    lax.fori_loop(0, blocks, attend, 0)
+        return number
+
+    lax.fori_loop(0, blocks, attend, SUBS)
+    groups = [n // 4 + n % 4 // 2 + n % 2 for n in range(1, blocks + 1)]
+    attended = SUBS + sum(groups) + 2 * blocks + blocks // 2
     scatter_second(1, blocks - 1)
+    for index in range(slices):
+        cols = slice(index * LANES, (index + 1) * LANES)
+        for which, source in ((0, sum_out[:, cols]), (1, sum_qkv[:q_cols, cols])):
+            row = (2 * index + which) * q_cols
+            part[base + row // width, row % width : row % width + q_cols] = source.astype(BF)
+    ends = [(base, 0), (base + 1, 1), (base + 2, 0)]
+    for unit, kind in ends:
+        big.start(unit, kind, 0)
 
     def key_value(block, carry):
+        @pl.when(block < 2)
+        def _():
+            ring.slot(attended + block)
+
         lanes = pl.ds(pl.multiple_of(block * TILE, TILE), TILE)
         cosine, sine = table_ref[:HALF, lanes], table_ref[HALF:, lanes]
         gkv_all[block, :HD] = turn(d_key[:, lanes], cosine, -sine).astype(BF)
@@ -728,15 +770,7 @@
         owner = (t + hop + 1) % 4
         kv_copy(owner, hop, owner).start()
 
-    for index in range(slices):
-        cols = slice(index * LANES, (index + 1) * LANES)
-        for which, source in ((0, sum_out[:, cols]), (1, sum_qkv[:q_cols, cols])):
-            row = (2 * index + which) * q_cols
-            part[base + row // width, row % width : row % width + q_cols] = source.astype(BF)
-    part[base + 3] = sum_qkv[q_cols:].T.astype(BF)
-    ends = [(big, base + unit, unit % 2) for unit in range(4)] + [(small, 0, 0)]
-    for bundle, unit, kind in ends[:4]:
-        bundle.start(unit, kind, 0)
+    end_part[:width] = sum_qkv[q_cols:].T.astype(BF)
     row_sums = jnp.sum(bias_acc[: q_cols + 2 * HD], axis=1, keepdims=True)
     shift_one = jnp.sum(qkv_t[...].astype(F32) * row_sums, axis=0, keepdims=True)
     shift_two = norms_c[:, 5:6]
@@ -746,60 +780,117 @@
     lane = lax.broadcasted_iota(jnp.int32, (width, 8), 1)
     columns = jnp.where(lane == 0, gain_two, shift_two).T
     rows = jnp.concatenate([gain_one, shift_one, columns[:6]], axis=0)
-    part_small[0] = jnp.zeros(part_small.shape[1:], BF)
+    end_part[width:] = jnp.zeros((end_part.shape[0] - width, LANES), BF)
     for index in range(slices):
-        part_small[0, 16 * index : 16 * index + 8] = rows[
+        end_part[width + 16 * index : width + 16 * index + 8] = rows[
             :, index * LANES : (index + 1) * LANES
         ].astype(BF)
 
-    small.start(0, 0, 0)
-    lands = (tp_land, tp_land_small)
-
-    def tp_copy(index, sender, hop):
+    end_rows = end_part.shape[0] // RING
+
+    def end_chunk(index):
+        return pl.ds(pl.multiple_of(index * end_rows, 16), end_rows)
+
+    def end_copy(hop, gather):
+        peer = (spot + hop) % RING
+        done = end_total_ref.at[end_chunk(spot)]
         return pltpu.make_async_remote_copy(
-            src_ref=lands[index].at[sender],
-            dst_ref=lands[index].at[sender],
-            send_sem=tp_send.at[index, hop],
-            recv_sem=tp_recv.at[index, hop],
+            src_ref=done if gather else end_part.at[end_chunk(peer)],
+            dst_ref=done if gather else end_land.at[hop - 1],
+            send_sem=end_send.at[int(gather), hop - 1],
+            recv_sem=end_recv.at[int(gather), hop - 1],
+            device_id=(first_of_ring + peer, t),
+            device_id_type=MESH,
+        )
+
+    def end_exchange(index):
+        return pltpu.make_async_remote_copy(
+            src_ref=end_part.at[end_chunk(spot)],
+            dst_ref=end_swap.at[index],
+            send_sem=end_send.at[2, index],
+            recv_sem=end_recv.at[2, index],
+            device_id=(extra_peers[index], t),
+            device_id_type=MESH,
+        )
+
+    def tp_copy(sender, hop):
+        return pltpu.make_async_remote_copy(
+            src_ref=tp_land.at[sender],
+            dst_ref=tp_land.at[sender],
+            send_sem=tp_send.at[hop],
+            recv_sem=tp_recv.at[hop],
             device_id=(d, (t + hop + 1) % 4),
             device_id_type=MESH,
         )
 
-    middle_stage = 2 + len(plan.extra)
-    ring_slots = list(range(3 * blocks + 2, plan.slots))
-    for beat in range(plan.stages + 1):
+    hops = range(1, RING)
+    stores = [
+        pltpu.make_async_copy(source, target, store_sem.at[index])
+        for index, (source, target) in enumerate(
+            (
+                (block_out_ref, block_out_hbm),
+                (grad_tokens_ref, grad_tokens_hbm),
+                (total_ref.at[pl.ds(0, base)], total_hbm.at[pl.ds(0, base)]),
+                (total_ref.at[pl.ds(base, 3)], total_hbm.at[pl.ds(base, 3)]),
+                (end_total_ref, end_total_hbm),
+            )
+        )
+    ]
+    for hop in hops:
+        end_copy(hop, False).start()
+
+    def end_reduced():
+        for hop in hops:
+            end_copy(hop, False).wait()
+        summed = end_part[end_chunk(spot)].astype(F32)
+        for hop in hops:
+            summed = summed + end_land[hop - 1].astype(F32)
+        for index in range(len(plan.extra)):
+            end_part[end_chunk(spot)] = summed.astype(BF)
+            end_exchange(index).start()
+            end_exchange(index).wait()
+            summed = summed.astype(BF).astype(F32) + end_swap[index].astype(F32)
+        tp_land[t] = summed.astype(BF)
+        for hop in range(3):
+            tp_copy(t, hop).start()
+
+    def end_shared():
+        for hop in range(3):
+            tp_copy((t + 3 - hop) % 4, hop).wait_recv()
+        land = [tp_land[sender].astype(F32) for sender in range(4)]
+        end_total_ref[end_chunk(spot)] = (land[0] + land[1] + land[2] + land[3]).astype(BF)
+        for hop in hops:
+            end_copy(hop, True).start()
+
+    ring_slots = list(range(attended + 2, plan.slots))
+    for beat in range(max(plan.stages, 1 + (len(ring_slots) + 1) // 2)):
         for index in ring_slots[2 * beat : 2 * beat + 2]:
             ring.slot(index)
-        for index, (bundle, unit, kind) in enumerate(ends):
-            rows = pl.ds(*bundle.span(kind, 3))
-            shared = index - 3
-            if shared < 0 or beat < middle_stage:
-                if beat < plan.stages:
-                    bundle.finish(unit, kind, beat)
+        if beat < plan.stages:
+            for unit, kind in ends:
+                big.finish(unit, kind, beat)
                 if beat + 1 < plan.stages:
-                    bundle.start(unit, kind, beat + 1)
-            elif beat == middle_stage:
-                bundle.finish(unit, kind, beat, publish=False)
-                lands[shared][t] = bundle.part[unit, rows]
-                for hop in range(3):
-                    tp_copy(shared, t, hop).start()
-            elif beat == middle_stage + 1:
-                for hop in range(3):
-                    tp_copy(shared, (t + 3 - hop) % 4, hop).wait_recv()
-                land = [lands[shared][sender].astype(F32) for sender in range(4)]
-                bundle.total[unit, rows] = (land[0] + land[1] + land[2] + land[3]).astype(BF)
-                bundle.start(unit, kind, beat)
-            else:
-                bundle.finish(unit, kind, beat - 1)
-                if beat < plan.stages:
-                    bundle.start(unit, kind, beat)
-        if 0 < beat <= own_blocks:
-            emit_block_out(beat - 1)
-        elif 4 <= beat < 4 + own_blocks:
-            emit_grad_tokens(beat - 4)
-    for index in range(2):
-        for hop in range(3):
-            tp_copy(index, t, hop).wait_send()
+                    big.start(unit, kind, beat + 1)
+        if beat == 0:
+            emit_block_out(0)
+        if beat == 1:
+            end_reduced()
+            emit_block_out(1)
+            stores[0].start()
+        if beat == 2:
+            end_shared()
+            emit_grad_tokens(0)
+        if beat == 3:
+            emit_grad_tokens(1)
+            stores[1].start()
+        if beat == (len(ring_slots) + 1) // 2:
+            stores[2].start()
+    for hop in hops:
+        end_copy(hop, True).wait()
+    stores[3].start()
+    stores[4].start()
+    for hop in range(3):
+        tp_copy(t, hop).wait_send()
     for hop in range(3):
         kv_copy((t + hop + 1) % 4, hop, (t + hop + 1) % 4).wait_send()
 
@@ -809,6 +900,8 @@
         return carry
 
     lax.fori_loop(0, blocks, drain, 0)
+    for store in stores:
+        store.wait()
 
 
 def finish_kernel(
@@ -817,8 +910,7 @@
     down,
     up,
     ends,
-    keyval,
-    small,
+    shared,
     block_out_ref,
     grad_tokens_ref,
     grad_query_ref,
@@ -828,15 +920,19 @@
     grad_down_ref,
     *vector_refs,
 ):
+    width = down.shape[1]
     block_out_ref[...] = block_out_t[...].T
     grad_tokens_ref[...] = grad_tokens_t[...].T
-    grad_output_ref[...] = ends[0].astype(F32)
-    grad_query_ref[...] = ends[1].astype(F32)
-    grad_keyval_ref[...] = keyval[0].astype(F32)
-    grad_down_ref[...] = down[0].astype(F32)
-    grad_up_ref[...] = up[0].astype(F32)
+    grad_keyval_ref[...] = shared[:width].astype(F32)
+    for index in range(down.shape[0]):
+        cols = slice(index * LANES, (index + 1) * LANES)
+        grad_down_ref[:, cols] = down[index].astype(F32)
+        grad_up_ref[:, cols] = up[index].astype(F32)
+        grad_output_ref[:, cols] = ends[2 * index].astype(F32)
+        grad_query_ref[:, cols] = ends[2 * index + 1].astype(F32)
     for index, vector in enumerate(vector_refs):
-        rows = [small[0, 16 * k + index : 16 * k + index + 1] for k in range(pl.num_programs(0))]
+        starts = [width + 16 * k + index for k in range(width // LANES)]
+        rows = [shared[start : start + 1] for start in starts]
         vector[...] = jnp.concatenate(rows, axis=1).astype(F32).reshape(vector.shape)
 
 
@@ -868,12 +964,26 @@
     table = np.concatenate([np.cos(angles), np.sin(angles)], axis=0).astype(np.float32)
 
     slices = width // LANES
-    units = 2 * slices + 4
-    small_rows = LANES
+    units = 2 * slices + 3
+    end_rows = width + LANES
     extra = max(1, len(plan.extra))
     vmem = lambda *shape, kind=BF: pltpu.VMEM(shape, kind)
     dma = lambda *shape: pltpu.SemaphoreType.DMA(shape)
     scratch = [
+        vmem(own_len, width),
+        vmem(own_len, width),
+        vmem(q_cols, width),
+        vmem(width, kv_cols),
+        vmem(q_cols, width),
+        vmem(width, hidden),
+        vmem(hidden, width),
+        vmem(ROT, full_len, kind=F32),
+        vmem(width, own_len),
+        vmem(width, own_len),
+        vmem(units, width, LANES),
+        vmem(end_rows, LANES),
+        dma(8),
+        dma(5),
         vmem(2 * blocks, width, LANES),
         vmem(2 * blocks, width, LANES),
         vmem(2 * blocks, width, LANES),
@@ -905,11 +1015,10 @@
         vmem(units, width, LANES),
         vmem(units, width - width // 8, LANES),
         vmem(units, extra, width // 8, LANES),
-        vmem(1, small_rows, LANES),
-        vmem(1, small_rows - small_rows // 8, LANES),
-        vmem(1, extra, small_rows // 8, LANES),
-        vmem(4, width // 8, LANES),
-        vmem(4, small_rows // 8, LANES),
+        vmem(end_rows, LANES),
+        vmem(RING - 1, end_rows // RING, LANES),
+        vmem(extra, end_rows // RING, LANES),
+        vmem(4, end_rows // RING, LANES),
         vmem(2, blocks // 2, 2, width // 2, LANES),
         vmem(2, own_blocks, 2, width, LANES),
         vmem(2, own_blocks, 2, width, LANES),
@@ -919,29 +1028,30 @@
         dma(2, blocks),
         dma(2, blocks),
         dma(2, own_blocks, 2),
-        dma(4, plan.steps),
-        dma(4, plan.steps),
+        dma(2 * SUBS, plan.steps),
+        dma(2 * SUBS, plan.steps),
         dma(units, plan.stages),
         dma(units, plan.stages),
-        dma(1, plan.stages),
-        dma(1, plan.stages),
-        dma(2, 3),
-        dma(2, 3),
+        dma(3, RING - 1),
+        dma(3, RING - 1),
+        dma(3),
+        dma(3),
         dma(3),
         dma(3),
     ]
     in_vmem = pl.BlockSpec(memory_space=pltpu.VMEM)
+    anywhere = pl.BlockSpec(memory_space=pl.ANY)
     in_smem = pl.BlockSpec(memory_space=pltpu.SMEM)
-    block_out, grad_tokens, total, total_small = pl.pallas_call(
+    block_out, grad_tokens, total, end_total = pl.pallas_call(
         functools.partial(block_kernel, plan),
         out_shape=(
             jax.ShapeDtypeStruct((width, own_len), BF),
             jax.ShapeDtypeStruct((width, own_len), BF),
             jax.ShapeDtypeStruct((units, width, LANES), BF),
-            jax.ShapeDtypeStruct((1, small_rows, LANES), BF),
+            jax.ShapeDtypeStruct((end_rows, LANES), BF),
         ),
-        in_specs=[in_smem] * 2 + [in_vmem] * 12,
-        out_specs=(in_vmem,) * 4,
+        in_specs=[in_smem] * 2 + [anywhere] * 7 + [in_vmem] * 4 + [anywhere],
+        out_specs=(anywhere,) * 4,
         scratch_shapes=scratch,
         compiler_params=pltpu.CompilerParams(
             collective_id=0, has_side_effects=True, vmem_limit_bytes=63 << 20
@@ -976,21 +1086,21 @@
         ((width,), F32),
         ((width,), F32),
     )
-    by_columns = lambda rows: pl.BlockSpec((rows, LANES), lambda i: (0, i))
-    by_rows = pl.BlockSpec((LANES, own_len), lambda i: (i, 0))
+    group = 3
+    by_columns = lambda rows: pl.BlockSpec((rows, group * LANES), lambda i: (0, i))
+    by_rows = pl.BlockSpec((group * LANES, own_len), lambda i: (i, 0))
     block_out, grad_tokens, grad_query, grad_keyval, grad_output, grad_up, grad_down, *vectors = (
         pl.pallas_call(
             finish_kernel,
-            grid=(slices,),
+            grid=(slices // group,),
             out_shape=tuple(jax.ShapeDtypeStruct(*shape) for shape in finish_shapes),
             in_specs=[
                 by_rows,
                 by_rows,
-                pl.BlockSpec((1, width, LANES), lambda i: (i, 0, 0)),
-                pl.BlockSpec((1, width, LANES), lambda i: (slices + i, 0, 0)),
-                pl.BlockSpec((2, q_cols, LANES), lambda i: (first_end + i, 0, 0)),
-                pl.BlockSpec((1, width, LANES), lambda i: (2 * slices + 3, 0, 0)),
-                pl.BlockSpec((1, small_rows, LANES), lambda i: (0, 0, 0)),
+                pl.BlockSpec((group, width, LANES), lambda i: (i, 0, 0)),
+                pl.BlockSpec((group, width, LANES), lambda i: (slices // group + i, 0, 0)),
+                pl.BlockSpec((2 * group, q_cols, LANES), lambda i: (first_end // group + i, 0, 0)),
+                pl.BlockSpec((end_rows, LANES), lambda i: (0, 0)),
             ],
             out_specs=(
                 by_columns(own_len),
@@ -1012,8 +1122,7 @@
             total,
             total,
             total.reshape(units * width // q_cols, q_cols, LANES),
-            total,
-            total_small,
+            end_total,
         )
     )
     return (

time: 150 us -> 138 us (0.920)
  Pallas kernels: 149 us -> 136 us
    pallas_call x1, Pallas kernels: 141 us -> 131 us  [shards(): pl.pallas_call(functools.partial(block_kernel, plan), out_shape=(jax.Shap...]
    pallas_call x1, Pallas kernels: 7.35 us -> 5.39 us  [shards(): pl.pallas_call(finish_kernel, grid=(slices // group,), out_shape=tuple((j...]
where the time goes in v5:
time: 138 us
  Pallas kernels  136 us (99%)
  between operations  1.46 us (1%)
    pallas_call x1, Pallas kernels, shards(): pl.pallas_call(functools.partial(block_kernel, plan), out_shape=(jax.Shap...  131 us
    pallas_call x1, Pallas kernels, shards(): pl.pallas_call(finish_kernel, grid=(slices // group,), out_shape=tuple((j...  5.39 us

profile of v5, /device:TPU:0, one launch (start us, length us, event | category | flops | bytes accessed | tf_op | source)
XLA Modules:
  0.0 137.9 jit_solution(17301740399955871954)
XLA Ops:
  1.3 131.0 %shard_map.221 = (bf16[768,512]{1,0:T(8,128)(2,1)}, bf16[768,512]{1,0:T(8,128)(2,1)}, bf16[15,768,128]{2,1,0:T(8,128)(2,1)}, bf16[896,128]{1,0:T(8,128)(2,1)}) custom-call(s32[1]{0:T(128)S(6)} %copy.25.tags_ref, f32[8]{0:T(128)} %tag_weight_ref.1, bf16[512,768]{1,0:T(8,128)(2,1)} %bitcast.8, bf16[512,768]{1,0:T(8,128)(2,1)} %bitcast.9, ...), custom_call_target="tpu_custom_call" | custom-call | tf_op jit(solution)/shard_map/pallas_call | solution.py:1045
  132.4 5.4 %shard_map.222 = (bf16[512,768]{1,0:T(8,128)(2,1)}, bf16[512,768]{1,0:T(8,128)(2,1)}, f32[192,768]{1,0:T(8,128)}, f32[768,128]{1,0:T(8,128)}, f32[192,768]{1,0:T...) custom-call(bf16[768,512]{1,0:T(8,128)(2,1)} %get-tuple-element.26.b, ...), custom_call_target="tpu_custom_call" | custom-call | tf_op jit(solution)/shard_map/pallas_call | solution.py:1093

commit v6 on v5

--- a/solution.py
+++ b/solution.py
@@ -740,21 +740,18 @@
     for unit, kind in ends:
         big.start(unit, kind, 0)
 
-    def key_value(block, carry):
-        @pl.when(block < 2)
-        def _():
-            ring.slot(attended + block)
-
-        lanes = pl.ds(pl.multiple_of(block * TILE, TILE), TILE)
-        cosine, sine = table_ref[:HALF, lanes], table_ref[HALF:, lanes]
-        gkv_all[block, :HD] = turn(d_key[:, lanes], cosine, -sine).astype(BF)
-        gkv_all[block, HD:] = d_value[:, lanes].astype(BF)
-        grads = gkv_all[block]
-        bias_acc[q_cols : q_cols + 2 * HD] += grads[:, :LANES].astype(F32) + grads[:, LANES:].astype(F32)
-        sum_qkv[q_cols:] += mm_t(grads, pair(n1_all, block))
+    def key_value(step, carry):
+        for block in (2 * step, 2 * step + 1):
+            lanes = pl.ds(pl.multiple_of(block * TILE, TILE), TILE)
+            cosine, sine = table_ref[:HALF, lanes], table_ref[HALF:, lanes]
+            key_grads = turn(d_key[:, lanes], cosine, -sine)
+            grads = jnp.concatenate([key_grads, d_value[:, lanes]], axis=0).astype(BF)
+            gkv_all[block] = grads
+            bias_acc[q_cols : q_cols + 2 * HD] += grads[:, :LANES].astype(F32) + grads[:, LANES:].astype(F32)
+            sum_qkv[q_cols:] += mm_t(grads, pair(n1_all, block))
         return carry
 
-    lax.fori_loop(0, blocks, key_value, 0)
+    lax.fori_loop(0, blocks // 2, key_value, 0)
 
     def kv_copy(owner, hop, target):
         return pltpu.make_async_remote_copy(
@@ -862,15 +859,15 @@
         for hop in hops:
             end_copy(hop, True).start()
 
-    ring_slots = list(range(attended + 2, plan.slots))
+    ring_slots = list(range(attended, plan.slots))
     for beat in range(max(plan.stages, 1 + (len(ring_slots) + 1) // 2)):
-        for index in ring_slots[2 * beat : 2 * beat + 2]:
-            ring.slot(index)
         if beat < plan.stages:
             for unit, kind in ends:
                 big.finish(unit, kind, beat)
                 if beat + 1 < plan.stages:
                     big.start(unit, kind, beat + 1)
+        for index in ring_slots[2 * beat : 2 * beat + 2]:
+            ring.slot(index)
         if beat == 0:
             emit_block_out(0)
         if beat == 1:

time: 138 us -> 137 us (level)
  no operation moved by 1% of the time
where the time goes in v6:
time: 137 us
  Pallas kernels  135 us (99%)
  between operations  1.46 us (1%)
    pallas_call x1, Pallas kernels, shards(): pl.pallas_call(functools.partial(block_kernel, plan), out_shape=(jax.Shap...  130 us
    pallas_call x1, Pallas kernels, shards(): pl.pallas_call(finish_kernel, grid=(slices // group,), out_shape=tuple((j...  5.39 us

profile of v6, /device:TPU:0, one launch (start us, length us, event | category | flops | bytes accessed | tf_op | source)
XLA Modules:
  0.0 136.6 jit_solution(7155416800673139550)
XLA Ops:
  1.3 129.7 %shard_map.221 = (bf16[768,512]{1,0:T(8,128)(2,1)}, bf16[768,512]{1,0:T(8,128)(2,1)}, bf16[15,768,128]{2,1,0:T(8,128)(2,1)}, bf16[896,128]{1,0:T(8,128)(2,1)}) custom-call(s32[1]{0:T(128)S(6)} %copy.25.tags_ref, f32[8]{0:T(128)} %tag_weight_ref.1, bf16[512,768]{1,0:T(8,128)(2,1)} %bitcast.8, bf16[512,768]{1,0:T(8,128)(2,1)} %bitcast.9, ...), custom_call_target="tpu_custom_call" | custom-call | tf_op jit(solution)/shard_map/pallas_call | solution.py:1042
  131.0 5.4 %shard_map.222 = (bf16[512,768]{1,0:T(8,128)(2,1)}, bf16[512,768]{1,0:T(8,128)(2,1)}, f32[192,768]{1,0:T(8,128)}, f32[768,128]{1,0:T(8,128)}, f32[192,768]{1,0:T...) custom-call(bf16[768,512]{1,0:T(8,128)(2,1)} %get-tuple-element.26.b, ...), custom_call_target="tpu_custom_call" | custom-call | tf_op jit(solution)/shard_map/pallas_call | solution.py:1090

commit v7 on v6

--- a/solution.py
+++ b/solution.py
@@ -372,21 +372,21 @@
             device_id_type=MESH,
         )
 
-    loads[0].wait()
-    loads[1].wait()
     for piece in range(own_blocks):
-        rows = slice(piece * TILE, (piece + 1) * TILE)
-        put_pair(x_all, t * own_blocks + piece, tok_ref[rows, :].T)
         for half in range(2):
+            place = 2 * (t * own_blocks + piece) + half
+            first = piece * TILE + half * LANES
+            rows = slice(first, first + LANES)
+            if first == 0:
+                loads[0].wait()
+            x_all[place] = tok_ref[rows, :].T
+            gather_copy(0, piece, half, t, 1).start()
             gather_copy(0, piece, half, t, 0).start()
-        gather_copy(0, piece, 0, t, 1).start()
-        weighted = (cot_ref[rows, :].astype(F32) * row_weight).astype(BF).T
-        put_pair(gr_all, t * own_blocks + piece, weighted)
-        for half in range(2):
+            if first == 0:
+                loads[1].wait()
+            gr_all[place] = (cot_ref[rows, :].astype(F32) * row_weight).astype(BF).T
+            gather_copy(1, piece, half, t, 1).start()
             gather_copy(1, piece, half, t, 0).start()
-        gather_copy(1, piece, 0, t, 1).start()
-        gather_copy(0, piece, 1, t, 1).start()
-        gather_copy(1, piece, 1, t, 1).start()
 
     for load in loads[2:]:
         load.wait()

time: 137 us -> 137 us (level)
  no operation moved by 1% of the time
where the time goes in v7:
time: 137 us; the launch traced here: 136 us
  Pallas kernels  135 us (99%)
  between operations  1.46 us (1%)
    pallas_call x1, Pallas kernels, shards(): pl.pallas_call(functools.partial(block_kernel, plan), out_shape=(jax.Shap...  130 us
    pallas_call x1, Pallas kernels, shards(): pl.pallas_call(finish_kernel, grid=(slices // group,), out_shape=tuple((j...  5.39 us

profile of v7, /device:TPU:0, one launch (start us, length us, event | category | flops | bytes accessed | tf_op | source)
XLA Modules:
  0.0 136.5 jit_solution(8838524570279497200)
XLA Ops:
  1.3 129.6 %shard_map.221 = (bf16[768,512]{1,0:T(8,128)(2,1)}, bf16[768,512]{1,0:T(8,128)(2,1)}, bf16[15,768,128]{2,1,0:T(8,128)(2,1)}, bf16[896,128]{1,0:T(8,128)(2,1)}) custom-call(s32[1]{0:T(128)S(6)} %copy.25.tags_ref, f32[8]{0:T(128)} %tag_weight_ref.1, bf16[512,768]{1,0:T(8,128)(2,1)} %bitcast.8, bf16[512,768]{1,0:T(8,128)(2,1)} %bitcast.9, ...), custom_call_target="tpu_custom_call" | custom-call | tf_op jit(solution)/shard_map/pallas_call | solution.py:1042
  130.9 5.4 %shard_map.222 = (bf16[512,768]{1,0:T(8,128)(2,1)}, bf16[512,768]{1,0:T(8,128)(2,1)}, f32[192,768]{1,0:T(8,128)}, f32[768,128]{1,0:T(8,128)}, f32[192,768]{1,0:T...) custom-call(bf16[768,512]{1,0:T(8,128)(2,1)} %get-tuple-element.26.b, ...), custom_call_target="tpu_custom_call" | custom-call | tf_op jit(solution)/shard_map/pallas_call | solution.py:1090

commit v8 on v7

--- a/solution.py
+++ b/solution.py
@@ -868,16 +868,16 @@
                     big.start(unit, kind, beat + 1)
         for index in ring_slots[2 * beat : 2 * beat + 2]:
             ring.slot(index)
-        if beat == 0:
-            emit_block_out(0)
         if beat == 1:
             end_reduced()
+            emit_block_out(0)
+        if beat == 2:
+            end_shared()
             emit_block_out(1)
             stores[0].start()
-        if beat == 2:
-            end_shared()
+        if beat == 3:
             emit_grad_tokens(0)
-        if beat == 3:
+        if beat == 4:
             emit_grad_tokens(1)
             stores[1].start()
         if beat == (len(ring_slots) + 1) // 2:

time: 137 us -> 137 us (level)
  no operation moved by 1% of the time
where the time goes in v8:
time: 137 us; the launch traced here: 136 us
  Pallas kernels  135 us (99%)
  between operations  1.46 us (1%)
    pallas_call x1, Pallas kernels, shards(): pl.pallas_call(functools.partial(block_kernel, plan), out_shape=(jax.Shap...  130 us
    pallas_call x1, Pallas kernels, shards(): pl.pallas_call(finish_kernel, grid=(slices // group,), out_shape=tuple((j...  5.39 us

profile of v8, /device:TPU:0, one launch (start us, length us, event | category | flops | bytes accessed | tf_op | source)
XLA Modules:
  0.0 136.5 jit_solution(7254280985641703227)
XLA Ops:
  1.3 129.6 %shard_map.221 = (bf16[768,512]{1,0:T(8,128)(2,1)}, bf16[768,512]{1,0:T(8,128)(2,1)}, bf16[15,768,128]{2,1,0:T(8,128)(2,1)}, bf16[896,128]{1,0:T(8,128)(2,1)}) custom-call(s32[1]{0:T(128)S(6)} %copy.25.tags_ref, f32[8]{0:T(128)} %tag_weight_ref.1, bf16[512,768]{1,0:T(8,128)(2,1)} %bitcast.8, bf16[512,768]{1,0:T(8,128)(2,1)} %bitcast.9, ...), custom_call_target="tpu_custom_call" | custom-call | tf_op jit(solution)/shard_map/pallas_call | solution.py:1042
  130.9 5.4 %shard_map.222 = (bf16[512,768]{1,0:T(8,128)(2,1)}, bf16[512,768]{1,0:T(8,128)(2,1)}, f32[192,768]{1,0:T(8,128)}, f32[768,128]{1,0:T(8,128)}, f32[192,768]{1,0:T...) custom-call(bf16[768,512]{1,0:T(8,128)(2,1)} %get-tuple-element.26.b, ...), custom_call_target="tpu_custom_call" | custom-call | tf_op jit(solution)/shard_map/pallas_call | solution.py:1090
